TPU v7x, 128 devices: a whole 4x4x4 slice. The times are simulated.
128 devices in a mesh: row: 16 (over z_lo, y, core), col: 8 (over z_hi, x).
Axes of the slice: x: 4, y: 4, z: 4 (z_hi: 2, z_lo: 2; z = z_hi * 2 + z_lo), core: 2. Of those that a mesh axis runs over, the one named last changes fastest.
Arguments:
- a_values: float32 [8192, 8192], P('row', 'col'), may hold values from -6 to 6
- a_mask: int32 [64, 64], P('row', 'col'), may hold values from 0 to 1, as said below
- b_values: float32 [8192, 8192], P('row', 'col'), may hold values from -0.5 to 0.5
- b_mask: int32 [64, 64], P('row', 'col'), may hold values from 0 to 1, as said below
- keep: int32 [64, 64, 64], P('row', None, 'col'), may hold values from 0 to 1, as said below
Outputs:
- product: float32 [8192, 8192], P('row', 'col')
Inputs may be any that keep to these rules, and one draw needn't show every extreme that they name: `keep`: 0 means the triple is filtered out, 1 that it counts. `a_mask`: 1 means the block is stored; on one device at most 20 blocks are stored, and some device holds exactly 20. `b_mask`: 1 means the block is stored; on one device at most 20 blocks are stored, and some device holds exactly 20.
All inputs are finite; a program needn't handle non-finite values.
Results may differ from a plain program's by a relative error of at most 0.000071.
Values sent between devices are 32-bit elements; how exact they have to be, the bound alone decides.
No kernel may reach another device: no remote copies, remote signals or barrier semaphores. Data moves between devices by JAX's collectives and lax.ppermute only.
A program may use at most 384 MiB of HBM per device.

v0:
```python
import functools

import jax
import jax.numpy as jnp
import numpy as np
from jax import lax
from jax.experimental import pallas as pl
from jax.experimental.pallas import tpu as pltpu
from jax.sharding import Mesh
from jax.sharding import PartitionSpec as P

W = 128
SLOTS = 10
DATA = SLOTS * W
TILES = 2 * DATA
ROWS = TILES + 16
ROW = ("zl", "y", "core")
COL = ("zh", "x")


def pack_kernel(core_ref, am_ref, bm_ref, a_ref, b_ref, keep_ref, send_ref, sem):
    core = core_ref[0]
    row = lax.broadcasted_iota(jnp.int32, (8, W), 0)
    lane = lax.broadcasted_iota(jnp.int32, (8, W), 1)
    factors = (
        (am_ref, a_ref, lambda r, c: (row == c) & (lane // 8 == r)),
        (bm_ref, b_ref, lambda r, c: (row == r) & (lane % 8 == c)),
    )

    def copy(n, src, dst, r, c, cols, at):
        return pltpu.make_async_copy(
            src.at[pl.ds(r * W, W), pl.ds(c * W, W)], dst.at[pl.ds(at, W), :], sem.at[n * 32 + r * cols + c]
        )

    for n, (mask, src, spot) in enumerate(factors):
        rows, cols = mask.shape
        slot = jnp.int32(0)
        tile = jnp.zeros((8, W), jnp.float32)
        for r in range(rows):
            for c in range(cols):
                on = mask[r, c] != 0
                fits = on & (slot < 2 * SLOTS)
                at = pl.multiple_of(slot * W, W)
                for dst, here in ((keep_ref, core == n), (send_ref, core != n)):

                    @pl.when(fits & here)
                    def _():
                        copy(n, src, dst, r, c, cols, at).start()

                slot = slot + on.astype(jnp.int32)
                tile = jnp.where(spot(r, c), jnp.where(on, slot, 0).astype(jnp.float32), tile)
        flag = jnp.zeros((8, W), jnp.float32) + jnp.where(slot > SLOTS, 1.0, 0.0)
        for dst, here in ((keep_ref, core == n), (send_ref, core != n)):

            @pl.when(here)
            def _():
                dst[pl.ds(TILES, 8), :] = tile
                dst[pl.ds(TILES + 8, 8), :] = flag

    for n, (mask, src, _) in enumerate(factors):
        rows, cols = mask.shape
        for r in range(rows):
            for c in range(cols):

                @pl.when(mask[r, c] != 0)
                def _():
                    copy(n, src, keep_ref, r, c, cols, 0).wait()


def pack(core, a_mask, b_mask, a_values, b_values):
    smem = pl.BlockSpec(memory_space=pltpu.SMEM)
    vmem = pl.BlockSpec(memory_space=pltpu.VMEM)
    hbm = pl.BlockSpec(memory_space=pl.ANY)
    return pl.pallas_call(
        pack_kernel,
        out_shape=(jax.ShapeDtypeStruct((ROWS, W), jnp.float32),) * 2,
        in_specs=[smem, smem, smem, hbm, hbm],
        out_specs=(vmem,) * 2,
        scratch_shapes=[pltpu.SemaphoreType.DMA((64,))],
        name="pack",
    )(core, a_mask, b_mask, a_values, b_values)


def merge_kernel(core_ref, keep_ref, got_ref, main_ref, excess_ref):
    core = core_ref[0]
    for ref, at in ((keep_ref, core), (got_ref, 1 - core)):
        main_ref[pl.ds(pl.multiple_of(at * DATA, DATA), DATA), :] = ref[pl.ds(0, DATA), :]
        main_ref[pl.ds(pl.multiple_of(TILES + at * 8, 8), 8), :] = ref[pl.ds(TILES, 8), :]
    own = keep_ref[pl.ds(TILES + 8, 8), :]
    also = got_ref[pl.ds(TILES + 8, 8), :]
    kept = jnp.where(also[:1] > 0, got_ref[pl.ds(DATA, DATA), :], 0.0)
    excess_ref[pl.ds(0, DATA), :] = jnp.where(own[:1] > 0, keep_ref[pl.ds(DATA, DATA), :], kept)
    excess_ref[pl.ds(DATA, 8), :] = own + also


def merge(core, keep, got):
    vmem = pl.BlockSpec(memory_space=pltpu.VMEM)
    return pl.pallas_call(
        merge_kernel,
        out_shape=(
            jax.ShapeDtypeStruct((ROWS, W), jnp.float32),
            jax.ShapeDtypeStruct((DATA + 8, W), jnp.float32),
        ),
        in_specs=[pl.BlockSpec(memory_space=pltpu.SMEM), vmem, vmem],
        out_specs=(vmem, vmem),
        name="merge",
    )(core, keep, got)


def split(x):
    high = x.astype(jnp.bfloat16)
    low = (x - high.astype(jnp.float32)).astype(jnp.bfloat16)
    return high, low


def product_kernel(shapes, spread, where_ref, keep_ref, *refs):
    count = sum(shapes)
    pieces = list(refs[:count])
    out_ref, acc, a_all, b_all, a_meta, b_meta, table, words, table_s, words_s, list_s, sem, sem_t, sem_o = refs[count:]
    core = where_ref[0]
    groups = []
    for size in shapes:
        groups.append(pieces[:size])
        pieces = pieces[size:]
    lines, extra = groups[:17], groups[17:]

    def parts(piece):
        if len(piece) == 1:
            return [piece[0].at[pl.ds(0, DATA), :], piece[0].at[pl.ds(DATA, DATA), :], piece[0].at[pl.ds(TILES, 16), :]]
        return [piece[0], piece[1].at[pl.ds(0, DATA), :], piece[1].at[pl.ds(DATA, 16), :]]

    def copies(side):
        found = []
        for n in range(8):
            a_at, b_at = where_ref[1 + n], where_ref[9 + n]
            pair = (parts(lines[2 * n]), parts(lines[2 * n + 1]))
            a_parts, b_parts = pair[side], pair[1 - side]
            found.append((a_parts[side], a_all.at[pl.ds(a_at * DATA, DATA), :]))
            found.append((a_parts[2].at[pl.ds(8 * side, 8), :], a_meta.at[pl.ds(a_at * 8, 8), :]))
            for h in range(2):
                found.append((b_parts[h], b_all.at[pl.ds((b_at * 2 + h) * DATA, DATA), :]))
            found.append((b_parts[2], b_meta.at[pl.ds(b_at * 16, 16), :]))
        if not spread:
            e = lines[16]
            found.append((e[side].at[pl.ds(0, DATA), :], a_all.at[pl.ds(8 * DATA, DATA), :]))
            found.append((e[1 - side].at[pl.ds(0, DATA), :], b_all.at[pl.ds(16 * DATA, DATA), :]))
        for n, piece in enumerate(extra):
            if n < 8:
                found.append((piece[0], a_all.at[pl.ds((8 + where_ref[1 + n]) * DATA, DATA), :]))
            else:
                h = side if n < 16 else 1 - side
                at = 16 + where_ref[9 + n % 8] * 2 + h
                found.append((piece[0], b_all.at[pl.ds(at * DATA, DATA), :]))
        found.sort(key=lambda pair: pair[0].shape[0] >= DATA)
        small = sum(pair[0].shape[0] < DATA for pair in found)
        made = [pltpu.make_async_copy(src, dst, sem.at[n]) for n, (src, dst) in enumerate(found)]
        return made, made[:small], made[small:]

    for side in range(2):

        @pl.when(core == side)
        def _():
            for copy in copies(side)[0]:
                copy.start()

    def settle(which):
        for side in range(2):

            @pl.when(core == side)
            def _():
                for copy in copies(side)[which]:
                    copy.wait()

    acc[...] = jnp.zeros(acc.shape, jnp.float32)
    settle(1)

    def address(piece, rank, pieces):
        rest = pieces * SLOTS + rank - (SLOTS + 1)
        if spread:
            rest = rest + piece * SLOTS
        return jnp.where(rank <= SLOTS, piece * SLOTS + rank - 1, rest)

    k8 = lax.broadcasted_iota(jnp.int32, (8, W), 0)
    one = jnp.ones((8, W), jnp.int32)
    low = jnp.zeros((8, W), jnp.int32)
    high = jnp.zeros((8, W), jnp.int32)
    for c in range(8):
        a_slot = a_meta[pl.ds(c * 8, 8), :].astype(jnp.int32)
        b0 = b_meta[pl.ds(c * 16, 8), :].astype(jnp.int32)
        b1 = pltpu.roll(b_meta[pl.ds(c * 16 + 8, 8), :], 4, 0).astype(jnp.int32)
        b_slot = jnp.where(k8 < 4, b0, b1)
        live = (keep_ref[pl.ds(c * 8, 8), :] != 0) & (a_slot > 0) & (b_slot > 0)
        a_at = address(c, a_slot, 8)
        b_at = address(jnp.where(k8 < 4, 2 * c, 2 * c + 1), b_slot, 16)
        table[pl.ds(c * 8, 8), :] = jnp.where(live, a_at + b_at * 65536, 0)
        bit = jnp.where(live, lax.shift_left(one, k8 + 8 * (c % 4)), 0)
        if c < 4:
            low = low | bit
        else:
            high = high | bit
    for n, word in enumerate((low, high)):
        word = word | pltpu.roll(word, 4, 0)
        word = word | pltpu.roll(word, 2, 0)
        word = word | pltpu.roll(word, 1, 0)
        words[pl.ds(8 * n, 8), :] = jnp.where(k8 == 0, word, lax.population_count(word))
    t0 = pltpu.make_async_copy(table, table_s, sem_t.at[0])
    t1 = pltpu.make_async_copy(words, words_s, sem_t.at[1])
    t0.start()
    t1.start()
    t0.wait()
    t1.wait()

    def gather(p, total):
        for n in range(2):

            def one(m, bits):
                lowest = bits & -bits
                k = 31 - lax.clz(lowest) + 32 * n
                list_s[0, total + m] = table_s[k, p]
                list_s[1, total + m] = p
                return bits ^ lowest

            found = words_s[8 * n + 1, p]
            lax.fori_loop(0, found, one, words_s[8 * n, p])
            total = total + found
        return total

    def term(entry):
        a_at = pl.multiple_of((entry & 65535) * W, W)
        b_at = pl.multiple_of(lax.shift_right_logical(entry, 16) * W, W)
        a_high, a_low = split(a_all[pl.ds(a_at, W), :])
        b_high, b_low = split(b_all[pl.ds(b_at, W), :])
        left = jnp.concatenate([a_high, a_low], axis=1)
        right = jnp.concatenate(
            [jnp.concatenate([b_high, b_low], axis=1), jnp.concatenate([b_low, b_high], axis=1)], axis=0
        )
        both = jnp.dot(left, right, preferred_element_type=jnp.float32)
        return both[:, :W] + both[:, W:]

    def place(p):
        return pl.ds(pl.multiple_of(p // 8 * W, W), W), pl.ds(pl.multiple_of(p % 8 * W, W), W)

    total = lax.fori_loop(0, 32, gather, jnp.int32(0))
    settle(2)

    def four(t, _):
        terms = [term(list_s[0, 4 * t + n]) for n in range(4)]
        for n in range(4):
            rows, cols = place(list_s[1, 4 * t + n])
            acc[rows, cols] = acc[rows, cols] + terms[n]
        return 0

    def single(t, _):
        rows, cols = place(list_s[1, t])
        acc[rows, cols] = acc[rows, cols] + term(list_s[0, t])
        return 0

    lax.fori_loop(0, total // 4, four, 0)
    lax.fori_loop(total // 4 * 4, total, single, 0)
    out = pltpu.make_async_copy(acc, out_ref, sem_o)
    out.start()
    out.wait()


def product(spread, where, keep_tile, groups):
    hbm = pl.BlockSpec(memory_space=pl.ANY)
    shapes = tuple(len(group) for group in groups)
    pieces = [piece for group in groups for piece in group]
    more = (8, 16) if spread else (1, 1)
    return pl.pallas_call(
        functools.partial(product_kernel, shapes, spread),
        out_shape=jax.ShapeDtypeStruct((512, 1024), jnp.float32),
        in_specs=[pl.BlockSpec(memory_space=pltpu.SMEM), pl.BlockSpec(memory_space=pltpu.VMEM)] + [hbm] * len(pieces),
        out_specs=hbm,
        scratch_shapes=[
            pltpu.VMEM((512, 1024), jnp.float32),
            pltpu.VMEM(((8 + more[0]) * DATA, W), jnp.float32),
            pltpu.VMEM(((16 + more[1]) * DATA, W), jnp.float32),
            pltpu.VMEM((64, W), jnp.float32),
            pltpu.VMEM((128, W), jnp.float32),
            pltpu.VMEM((64, W), jnp.int32),
            pltpu.VMEM((16, W), jnp.int32),
            pltpu.SMEM((64, W), jnp.int32),
            pltpu.SMEM((16, W), jnp.int32),
            pltpu.SMEM((2, 2048), jnp.int32),
            pltpu.SemaphoreType.DMA((72,)),
            pltpu.SemaphoreType.DMA((2,)),
            pltpu.SemaphoreType.DMA,
        ],
        compiler_params=pltpu.CompilerParams(vmem_limit_bytes=(40 if spread else 24) * 1024 * 1024),
        name="product",
    )(where, keep_tile, *pieces)


def swap(x, axis):
    return lax.ppermute(x, axis, [(0, 1), (1, 0)])


def right(x, axis):
    return lax.ppermute(x, axis, [(n, (n + 1) % 4) for n in range(4)])


def left(x, axis):
    return lax.ppermute(x, axis, [(n, (n - 1) % 4) for n in range(4)])


def opposite(from_left, from_right, core, axis):
    if axis == "x":
        axes, at = ("core", "x"), lambda n, c: c * 4 + n % 4
    else:
        axes, at = ("y", "core"), lambda n, c: n % 4 * 2 + c
    pairs = [(at(n, c), at(n + 1 - 2 * c, c)) for n in range(4) for c in range(2)]
    return lax.ppermute(jnp.where(core == 0, from_left, from_right), axes, pairs)


def gate(*done):
    return lambda x: lax.optimization_barrier((x, *done))[0]


def around(own, z, axis, core):
    other = swap(own, z)
    found = []
    for x in (own, other):
        r, l = right(x, axis), left(x, axis)
        found.extend((x, r, l, opposite(r, l, core, axis)))
    return found


SIZES = (2, 4, 2, 2, 4)


def route(x, ring, z):
    pairs = []
    for n in range(128):
        zl, y, core, zh, at = (int(i) for i in np.unravel_index(n, SIZES))
        if core == 0:
            to = (zl, y, core, zh ^ z, ring(at))
        else:
            to = (zl ^ z, ring(y), core, zh, at)
        pairs.append((n, int(np.ravel_multi_index(to, SIZES))))
    return lax.ppermute(x, ROW + COL, pairs)


def forth(x):
    return route(x, lambda n: (n + 1) % 4, 0)


def back(x):
    return route(x, lambda n: (n - 1) % 4, 0)


def cross(x):
    return route(x, lambda n: n, 1)


def pair(x, distance):
    return route(x, lambda n: n ^ distance, 0)


def per_device(a_values, a_mask, b_values, b_mask, keep):
    zl, y, core = (lax.axis_index(n) for n in ROW)
    zh, x = (lax.axis_index(n) for n in COL)
    core_s = core.reshape(1).astype(jnp.int32)
    keep_tile = jnp.pad(jnp.transpose(keep, (1, 0, 2)).reshape(64, 32), ((0, 0), (0, W - 32)))
    held, sent = pack(core_s, a_mask, b_mask, a_values, b_values)
    m, e = merge(core_s, held, swap(sent, "core"))

    z0 = cross(m[:DATA])
    r, l = forth(m), back(m)
    e1 = pair(e, 1)
    cm = swap(m, "core")

    g = gate(r, l)
    z1 = cross(g(m[DATA:]))
    o0, o1 = forth(g(r[:DATA])), back(g(l[DATA:]))
    z0r, z0l = forth(g(z0)), back(g(z0))
    e = gate(o0, o1)(e) + e1
    e2 = pair(e, 2)
    cr, cl = swap(r, "core"), swap(l, "core")

    g = gate(z1, z0r, z0l)
    z1r, z1l = forth(g(z1)), back(g(z1))
    zo0 = forth((z0r))
    e = g(e) + e2
    e3 = cross(e)
    cz0, co0, co1 = swap(z0, "core"), swap(o0, "core"), swap(o1, "core")
    cz0r, cz0l = swap(z0r, "core"), swap(z0l, "core")

    g = gate(z1r, z1l, cm, cr, cl, co0, co1, cz0)
    zo1 = back(g(z1l))
    e = g(e) + e3
    cz1, cz1r, cz1l = swap(z1, "core"), swap(z1r, "core"), swap(z1l, "core")
    czo0 = swap(zo0, "core")
    ce = swap(e, "core")
    czo1 = swap(zo1, "core")

    shifts = (0, 3, 1, 2)
    groups = [[m], [cm], [r], [cr], [l], [cl], [o0, o1], [co0, co1]]
    groups += [[z0, z1], [cz0, cz1], [z0r, z1r], [cz0r, cz1r], [z0l, z1l], [cz0l, cz1l], [zo0, zo1], [czo0, czo1], [e, ce]]
    where = [core] + [(zh ^ n) * 4 + (x + s) % 4 for n in range(2) for s in shifts]
    where += [(zl ^ n) * 4 + (y + s) % 4 for n in range(2) for s in shifts]
    where = jnp.stack(where).astype(jnp.int32)
    crowd = [q[DATA, 0] > 1.5 for q in (e, ce)]

    def few(_):
        return product(False, where, keep_tile, groups)

    def many(_):
        first = core == 0
        crowd_a, crowd_b = jnp.where(first, crowd[0], crowd[1]), jnp.where(first, crowd[1], crowd[0])
        rest_a = jnp.where(first, held, sent)[DATA:TILES]
        rest_b = jnp.where(first, sent, held)[DATA:TILES]
        some_a = jnp.where(first, e, ce)[:DATA]
        some_b = jnp.where(first, ce, e)[:DATA]

        def all_b(_):
            found = around(rest_b, "zl", "y", core)
            return tuple(found + [swap(p, "core") for p in found])

        more = lax.cond(crowd_a, lambda _: tuple(around(rest_a, "zh", "x", core)), lambda _: (some_a,) * 8, 0)
        more += lax.cond(crowd_b, all_b, lambda _: (some_b,) * 16, 0)
        return product(True, where, keep_tile, groups + [[p] for p in more])

    return lax.cond(crowd[0] | crowd[1], many, few, 0)


def solution(mesh):
    fine = Mesh(mesh.devices.reshape(2, 4, 2, 2, 4), ROW + COL)
    return jax.shard_map(
        per_device,
        mesh=fine,
        in_specs=(P(ROW, COL), P(ROW, COL), P(ROW, COL), P(ROW, COL), P(ROW, None, COL)),
        out_specs=P(ROW, COL),
        check_vma=False,
    )
```

profile of v0, /device:TPU:1, one launch (start us, length us, event | category | flops | bytes accessed | tf_op | source)
XLA Modules:
  0.0 104.0 jit_solution(11374100550438109122)
XLA Ops:
  0.0 3.6 %pack.1 = (f32[2576,128]{1,0:T(8,128)S(1)}, f32[2576,128]{1,0:T(8,128)}) custom-call(s32[1]{0:T(128)} %bitcast.core_ref, s32[4,8]{1,0:T(4,128)} %am_ref.1, s32[4,8]{1,0:T(4,128)} %bm_ref.1, f32[512,1024]{1,0:T(8,128)} %a_ref.1, f32[512,1024]{1,0:T(8,128)} %b_ref.1), custom_call_target="tpu_custom_call" | custom-call | tf_op jit(solution)/shard_map/pack/pallas_call | solution.py:74
  3.7 1.6 %collective-permute-start.22 = (f32[2576,128]{1,0:T(8,128)}, f32[2576,128]{1,0:T(8,128)S(1)}, u32[]{:S(2)}, u32[]{:S(2)}) collective-permute-start(f32[2576,128]{1,0:T(8,128)} %get-tuple-element.295), channel_id=1, source_target_pairs={{0,8},{8,0},{1,9},{9,1},{2,10},{10,2},{3,11},{11,3},{4,12},{12,4},... | collective-permute-start | bytes 3956744 | tf_op jit(solution)/shard_map/ppermute | solution.py:296
  5.2 2.9 %collective-permute-done.22.got_ref = f32[2576,128]{1,0:T(8,128)S(1)} collective-permute-done((f32[2576,128]{1,0:T(8,128)}, f32[2576,128]{1,0:T(8,128)S(1)}, u32[]{:S(2)}, u32[]{:S(2)}) %collective-permute-start.22) | collective-permute-done | bytes 1318944 | tf_op jit(solution)/shard_map/ppermute | solution.py:296
  9.2 2.4 %merge.1 = (f32[2576,128]{1,0:T(8,128)S(1)}, f32[1288,128]{1,0:T(8,128)}) custom-call(s32[1]{0:T(128)} %bitcast.core_ref, f32[2576,128]{1,0:T(8,128)S(1)} %get-tuple-element.294.keep_ref, f32[2576,128]{1,0:T(8,128)} %copy-done.15), custom_call_target="tpu_custom_call" | custom-call | tf_op jit(solution)/shard_map/merge/pallas_call | solution.py:98
  11.5 1.3 %collective-permute-start.23 = (f32[2576,128]{1,0:T(8,128)S(1)}, f32[2576,128]{1,0:T(8,128)S(1)}, u32[]{:S(2)}, u32[]{:S(2)}) collective-permute-start(f32[2576,128]{1,0:T(8,128)S(1)} %get-tuple-element.297), channel_id=1, source_target_pairs={{0,1},{1,2},{2,3},{3,0},{4,5},{5,6},{6,7},{7,4},{8,24},{9,25},{10,... | collective-permute-start | bytes 3956744 | tf_op jit(solution)/shard_map/ppermute | solution.py:341
  12.8 1.4 %collective-permute-start.24 = (f32[2576,128]{1,0:T(8,128)S(1)}, f32[2576,128]{1,0:T(8,128)S(1)}, u32[]{:S(2)}, u32[]{:S(2)}) collective-permute-start(f32[2576,128]{1,0:T(8,128)S(1)} %get-tuple-element.297), channel_id=1, source_target_pairs={{0,3},{1,0},{2,1},{3,2},{4,7},{5,4},{6,5},{7,6},{8,56},{9,57},{10,... | collective-permute-start | bytes 3956744 | tf_op jit(solution)/shard_map/ppermute | solution.py:341
  14.3 1.8 %collective-permute-start.29 = (f32[1280,128]{1,0:T(8,128)S(1)}, f32[1280,128]{1,0:T(8,128)S(1)}, u32[]{:S(2)}, u32[]{:S(2)}) collective-permute-start(f32[1280,128]{1,0:T(8,128)S(1)} %slice.41), channel_id=1, source_target_pairs={{0,4},{1,5},{2,6},{3,7},{4,0},{5,1},{6,2},{7,3},{8,72},{9,73},{10,... | collective-permute-start | bytes 1966088 | tf_op jit(solution)/shard_map/ppermute | solution.py:341
  16.1 11.2 %collective-permute-done.29 = f32[1280,128]{1,0:T(8,128)S(1)} collective-permute-done((f32[1280,128]{1,0:T(8,128)S(1)}, f32[1280,128]{1,0:T(8,128)S(1)}, u32[]{:S(2)}, u32[]{:S(2)}) %collective-permute-start.29) | collective-permute-done | bytes 655392 | tf_op jit(solution)/shard_map/ppermute | solution.py:341
  27.3 7.2 %collective-permute-start.40 = (f32[1280,128]{1,0:T(8,128)S(1)}, f32[1280,128]{1,0:T(8,128)S(1)}, u32[]{:S(2)}, u32[]{:S(2)}) collective-permute-start(f32[1280,128]{1,0:T(8,128)S(1)} %collective-permute-done.29), channel_id=1, source_target_pairs={{0,8},{8,0},{1,9},{9,1},{2,10},{10,2},{3,11},{11,3},{4,12},{12,4},... | collective-permute-start | bytes 1966088 | tf_op jit(solution)/shard_map/ppermute | solution.py:296
  35.3 2.2 %collective-permute-start.26 = (f32[1296,128]{1,0:T(8,128)S(1)}, f32[1296,128]{1,0:T(8,128)S(1)}, u32[]{:S(2)}, u32[]{:S(2)}) collective-permute-start(f32[1296,128]{1,0:T(8,128)S(1)} %slice.53), channel_id=1, source_target_pairs={{0,3},{1,0},{2,1},{3,2},{4,7},{5,4},{6,5},{7,6},{8,56},{9,57},{10,... | collective-permute-start | bytes 1990664 | tf_op jit(solution)/shard_map/ppermute | solution.py:341
  38.8 6.9 %collective-permute-done.25 = f32[1280,128]{1,0:T(8,128)S(1)} collective-permute-done((f32[1280,128]{1,0:T(8,128)S(1)}, f32[1280,128]{1,0:T(8,128)S(1)}, u32[]{:S(2)}, u32[]{:S(2)}) %collective-permute-start.25) | collective-permute-done | bytes 655392 | tf_op jit(solution)/shard_map/ppermute | solution.py:341
  46.8 6.0 %collective-permute-done.30 = f32[1280,128]{1,0:T(8,128)S(1)} collective-permute-done((f32[1280,128]{1,0:T(8,128)S(1)}, f32[1280,128]{1,0:T(8,128)S(1)}, u32[]{:S(2)}, u32[]{:S(2)}) %collective-permute-start.30) | collective-permute-done | bytes 655392 | tf_op jit(solution)/shard_map/ppermute | solution.py:341
  53.7 1.9 %collective-permute-done.31 = f32[1280,128]{1,0:T(8,128)S(1)} collective-permute-done((f32[1280,128]{1,0:T(8,128)S(1)}, f32[1280,128]{1,0:T(8,128)S(1)}, u32[]{:S(2)}, u32[]{:S(2)}) %collective-permute-start.31) | collective-permute-done | bytes 655392 | tf_op jit(solution)/shard_map/ppermute | solution.py:341
  55.6 1.5 %collective-permute-start.37 = (f32[2576,128]{1,0:T(8,128)S(1)}, f32[2576,128]{1,0:T(8,128)S(1)}, u32[]{:S(2)}, u32[]{:S(2)}) collective-permute-start(f32[2576,128]{1,0:T(8,128)S(1)} %collective-permute-done.24), channel_id=1, source_target_pairs={{0,8},{8,0},{1,9},{9,1},{2,10},{10,2},{3,11},{11,3},{4,12},{12,4},... | collective-permute-start | bytes 3956744 | tf_op jit(solution)/shard_map/ppermute | solution.py:296
  57.8 2.9 %collective-permute-done.38 = f32[1280,128]{1,0:T(8,128)S(1)} collective-permute-done((f32[1280,128]{1,0:T(8,128)S(1)}, f32[1280,128]{1,0:T(8,128)S(1)}, u32[]{:S(2)}, u32[]{:S(2)}) %collective-permute-start.38) | collective-permute-done | bytes 655392 | tf_op jit(solution)/shard_map/ppermute | solution.py:296
  60.7 2.0 %collective-permute-start.34 = (f32[1296,128]{1,0:T(8,128)}, f32[1296,128]{1,0:T(8,128)}, u32[]{:S(2)}, u32[]{:S(2)}) collective-permute-start(f32[1296,128]{1,0:T(8,128)} %collective-permute-done.28), channel_id=1, source_target_pairs={{0,3},{1,0},{2,1},{3,2},{4,7},{5,4},{6,5},{7,6},{8,56},{9,57},{10,... | collective-permute-start | bytes 1990664 | tf_op jit(solution)/shard_map/ppermute | solution.py:341
  62.7 1.3 %collective-permute-done.32 = f32[1288,128]{1,0:T(8,128)S(1)} collective-permute-done((f32[1288,128]{1,0:T(8,128)S(1)}, f32[1288,128]{1,0:T(8,128)S(1)}, u32[]{:S(2)}, u32[]{:S(2)}) %collective-permute-start.32) | collective-permute-done | bytes 659488 | tf_op jit(solution)/shard_map/ppermute | solution.py:341
  64.1 2.1 %collective-permute-start.39 = (f32[1296,128]{1,0:T(8,128)S(1)}, f32[1296,128]{1,0:T(8,128)S(1)}, u32[]{:S(2)}, u32[]{:S(2)}) collective-permute-start(f32[1296,128]{1,0:T(8,128)S(1)} %collective-permute-done.26), channel_id=1, source_target_pairs={{0,8},{8,0},{1,9},{9,1},{2,10},{10,2},{3,11},{11,3},{4,12},{12,4},... | collective-permute-start | bytes 1990664 | tf_op jit(solution)/shard_map/ppermute | solution.py:296
  67.1 4.2 %collective-permute-done.33 = f32[1296,128]{1,0:T(8,128)} collective-permute-done((f32[1296,128]{1,0:T(8,128)}, f32[1296,128]{1,0:T(8,128)}, u32[]{:S(2)}, u32[]{:S(2)}) %collective-permute-start.33) | collective-permute-done | bytes 663584 | tf_op jit(solution)/shard_map/ppermute | solution.py:341
  71.3 2.8 %collective-permute-start.49 = (f32[1296,128]{1,0:T(8,128)}, f32[1296,128]{1,0:T(8,128)}, u32[]{:S(2)}, u32[]{:S(2)}) collective-permute-start(f32[1296,128]{1,0:T(8,128)} %collective-permute-done.34), channel_id=1, source_target_pairs={{0,3},{1,0},{2,1},{3,2},{4,7},{5,4},{6,5},{7,6},{8,56},{9,57},{10,... | collective-permute-start | bytes 1990664 | tf_op jit(solution)/shard_map/ppermute | solution.py:341
  75.4 7.9 %collective-permute-done.41 = f32[1288,128]{1,0:T(8,128)S(1)} collective-permute-done((f32[1288,128]{1,0:T(8,128)S(1)}, f32[1288,128]{1,0:T(8,128)S(1)}, u32[]{:S(2)}, u32[]{:S(2)}) %collective-permute-start.41) | collective-permute-done | bytes 659488 | tf_op jit(solution)/shard_map/ppermute | solution.py:341
  90.2 2.0 %collective-permute-done.50 = f32[1280,128]{1,0:T(8,128)} collective-permute-done((f32[1280,128]{1,0:T(8,128)}, f32[1280,128]{1,0:T(8,128)}, u32[]{:S(2)}, u32[]{:S(2)}) %collective-permute-start.50) | collective-permute-done | bytes 655392 | tf_op jit(solution)/shard_map/ppermute | solution.py:296
  92.3 11.6 %conditional.3 = (f32[512,1024]{1,0:T(8,128)}) conditional(s32[]{:T(128)} %convert_element_type.9, (s32[17]{0:T(128)S(1)}, s32[64,128]{0,1:T(8,128)S(1)}, f32[2576,128]{1,0:T(8,128)S(1)}, f32[2576,128]{1,0:T(8,128)}, f32[2576,128]{1,0:T(8,128)}, /*index=5*/f32[2576,128]{1,0:T(8,128)}, f32[2576,128]{1,0:T(8,128)}, f32[2576,128]{1,0:T(8,128)}, ...), branch_computations={%region_0.1_spmd, %region_1.6_spmd} | conditional | flops 983047 | bytes 69534936 | solution.py:424
  92.3 11.3 %product.2 = f32[512,1024]{1,0:T(8,128)} custom-call(s32[17]{0:T(128)S(1)} %get-tuple-element.178.where_ref, s32[64,128]{1,0:T(8,128)S(1)} %copy.9.keep_ref, f32[2576,128]{1,0:T(8,128)S(1)} %get-tuple-element.180.refs_0_, f32[2576,128]{1,0:T(8,128)} %get-tuple-element.181.refs_1_, f32[2576,128]{1,0:T(8,128)} %get-tuple-element.182.refs_2_, ...), custom_call_target="tpu_custom_call" | custom-call | tf_op jit(solution)/shard_map/cond/branch_0_fun/product/pallas_call | solution.py:270
  (88 shorter events, 13.7 us)
Async XLA Ops:
  11.5 23.0 %collective-permute-start.23 = (f32[2576,128]{1,0:T(8,128)S(1)}, f32[2576,128]{1,0:T(8,128)S(1)}, u32[]{:S(2)}, u32[]{:S(2)}) collective-permute-start(f32[2576,128]{1,0:T(8,128)S(1)} %get-tuple-element.297), channel_id=1, source_target_pairs={{0,1},{1,2},{2,3},{3,0},{4,5},{5,6},{6,7},{7,4},{8,24},{9,25},{10,... | collective-permute-start | bytes 3956744 | tf_op jit(solution)/shard_map/ppermute | solution.py:341
  12.8 21.8 %collective-permute-start.24 = (f32[2576,128]{1,0:T(8,128)S(1)}, f32[2576,128]{1,0:T(8,128)S(1)}, u32[]{:S(2)}, u32[]{:S(2)}) collective-permute-start(f32[2576,128]{1,0:T(8,128)S(1)} %get-tuple-element.297), channel_id=1, source_target_pairs={{0,3},{1,0},{2,1},{3,2},{4,7},{5,4},{6,5},{7,6},{8,56},{9,57},{10,... | collective-permute-start | bytes 3956744 | tf_op jit(solution)/shard_map/ppermute | solution.py:341
  14.3 13.0 %collective-permute-start.29 = (f32[1280,128]{1,0:T(8,128)S(1)}, f32[1280,128]{1,0:T(8,128)S(1)}, u32[]{:S(2)}, u32[]{:S(2)}) collective-permute-start(f32[1280,128]{1,0:T(8,128)S(1)} %slice.41), channel_id=1, source_target_pairs={{0,4},{1,5},{2,6},{3,7},{4,0},{5,1},{6,2},{7,3},{8,72},{9,73},{10,... | collective-permute-start | bytes 1966088 | tf_op jit(solution)/shard_map/ppermute | solution.py:341
  16.1 22.1 %collective-permute-start.27 = (f32[1288,128]{1,0:T(8,128)}, f32[1288,128]{1,0:T(8,128)S(1)}, u32[]{:S(2)}, u32[]{:S(2)}) collective-permute-start(f32[1288,128]{1,0:T(8,128)} %get-tuple-element.300), channel_id=1, source_target_pairs={{0,1},{1,0},{2,3},{3,2},{4,5},{5,4},{6,7},{7,6},{8,24},{9,25},{10,... | collective-permute-start | bytes 1978376 | tf_op jit(solution)/shard_map/ppermute | solution.py:341
  27.3 11.1 %collective-permute-start.40 = (f32[1280,128]{1,0:T(8,128)S(1)}, f32[1280,128]{1,0:T(8,128)S(1)}, u32[]{:S(2)}, u32[]{:S(2)}) collective-permute-start(f32[1280,128]{1,0:T(8,128)S(1)} %collective-permute-done.29), channel_id=1, source_target_pairs={{0,8},{8,0},{1,9},{9,1},{2,10},{10,2},{3,11},{11,3},{4,12},{12,4},... | collective-permute-start | bytes 1966088 | tf_op jit(solution)/shard_map/ppermute | solution.py:296
  34.6 11.1 %collective-permute-start.25 = (f32[1280,128]{1,0:T(8,128)S(1)}, f32[1280,128]{1,0:T(8,128)S(1)}, u32[]{:S(2)}, u32[]{:S(2)}) collective-permute-start(f32[1280,128]{1,0:T(8,128)S(1)} %slice.52), channel_id=1, source_target_pairs={{0,1},{1,2},{2,3},{3,0},{4,5},{5,6},{6,7},{7,4},{8,24},{9,25},{10,... | collective-permute-start | bytes 1966088 | tf_op jit(solution)/shard_map/ppermute | solution.py:341
  35.3 11.3 %collective-permute-start.26 = (f32[1296,128]{1,0:T(8,128)S(1)}, f32[1296,128]{1,0:T(8,128)S(1)}, u32[]{:S(2)}, u32[]{:S(2)}) collective-permute-start(f32[1296,128]{1,0:T(8,128)S(1)} %slice.53), channel_id=1, source_target_pairs={{0,3},{1,0},{2,1},{3,2},{4,7},{5,4},{6,5},{7,6},{8,56},{9,57},{10,... | collective-permute-start | bytes 1990664 | tf_op jit(solution)/shard_map/ppermute | solution.py:341
  37.5 20.2 %collective-permute-start.35 = (f32[2576,128]{1,0:T(8,128)S(1)}, f32[2576,128]{1,0:T(8,128)S(1)}, u32[]{:S(2)}, u32[]{:S(2)}) collective-permute-start(f32[2576,128]{1,0:T(8,128)S(1)} %get-tuple-element.297), channel_id=1, source_target_pairs={{0,8},{8,0},{1,9},{9,1},{2,10},{10,2},{3,11},{11,3},{4,12},{12,4},... | collective-permute-start | bytes 3956744 | tf_op jit(solution)/shard_map/ppermute | solution.py:296
  38.2 18.9 %collective-permute-start.28 = (f32[1296,128]{1,0:T(8,128)S(1)}, f32[1296,128]{1,0:T(8,128)}, u32[]{:S(2)}, u32[]{:S(2)}) collective-permute-start(f32[1296,128]{1,0:T(8,128)S(1)} %slice.40), channel_id=1, source_target_pairs={{0,4},{1,5},{2,6},{3,7},{4,0},{5,1},{6,2},{7,3},{8,72},{9,73},{10,... | collective-permute-start | bytes 1990664 | tf_op jit(solution)/shard_map/ppermute | solution.py:341
  38.5 14.3 %collective-permute-start.30 = (f32[1280,128]{1,0:T(8,128)S(1)}, f32[1280,128]{1,0:T(8,128)S(1)}, u32[]{:S(2)}, u32[]{:S(2)}) collective-permute-start(f32[1280,128]{1,0:T(8,128)S(1)} %collective-permute-done.29), channel_id=1, source_target_pairs={{0,1},{1,2},{2,3},{3,0},{4,5},{5,6},{6,7},{7,4},{8,24},{9,25},{10,... | collective-permute-start | bytes 1966088 | tf_op jit(solution)/shard_map/ppermute | solution.py:341
  45.7 9.8 %collective-permute-start.31 = (f32[1280,128]{1,0:T(8,128)S(1)}, f32[1280,128]{1,0:T(8,128)S(1)}, u32[]{:S(2)}, u32[]{:S(2)}) collective-permute-start(f32[1280,128]{1,0:T(8,128)S(1)} %collective-permute-done.29), channel_id=1, source_target_pairs={{0,3},{1,0},{2,1},{3,2},{4,7},{5,4},{6,5},{7,6},{8,56},{9,57},{10,... | collective-permute-start | bytes 1966088 | tf_op jit(solution)/shard_map/ppermute | solution.py:341
  46.6 19.7 %collective-permute-start.36 = (f32[2576,128]{1,0:T(8,128)S(1)}, f32[2576,128]{1,0:T(8,128)S(1)}, u32[]{:S(2)}, u32[]{:S(2)}) collective-permute-start(f32[2576,128]{1,0:T(8,128)S(1)} %collective-permute-done.23), channel_id=1, source_target_pairs={{0,8},{8,0},{1,9},{9,1},{2,10},{10,2},{3,11},{11,3},{4,12},{12,4},... | collective-permute-start | bytes 3956744 | tf_op jit(solution)/shard_map/ppermute | solution.py:296
  52.7 11.3 %collective-permute-start.32 = (f32[1288,128]{1,0:T(8,128)S(1)}, f32[1288,128]{1,0:T(8,128)S(1)}, u32[]{:S(2)}, u32[]{:S(2)}) collective-permute-start(f32[1288,128]{1,0:T(8,128)S(1)} %add.116), channel_id=1, source_target_pairs={{0,2},{1,3},{2,0},{3,1},{4,6},{5,7},{6,4},{7,5},{8,40},{9,41},{10,... | collective-permute-start | bytes 1978376 | tf_op jit(solution)/shard_map/ppermute | solution.py:341
  55.6 11.5 %collective-permute-start.37 = (f32[2576,128]{1,0:T(8,128)S(1)}, f32[2576,128]{1,0:T(8,128)S(1)}, u32[]{:S(2)}, u32[]{:S(2)}) collective-permute-start(f32[2576,128]{1,0:T(8,128)S(1)} %collective-permute-done.24), channel_id=1, source_target_pairs={{0,8},{8,0},{1,9},{9,1},{2,10},{10,2},{3,11},{11,3},{4,12},{12,4},... | collective-permute-start | bytes 3956744 | tf_op jit(solution)/shard_map/ppermute | solution.py:296
  57.7 13.6 %collective-permute-start.33 = (f32[1296,128]{1,0:T(8,128)}, f32[1296,128]{1,0:T(8,128)}, u32[]{:S(2)}, u32[]{:S(2)}) collective-permute-start(f32[1296,128]{1,0:T(8,128)} %collective-permute-done.28), channel_id=1, source_target_pairs={{0,1},{1,2},{2,3},{3,0},{4,5},{5,6},{6,7},{7,4},{8,24},{9,25},{10,... | collective-permute-start | bytes 1990664 | tf_op jit(solution)/shard_map/ppermute | solution.py:341
  60.7 10.5 %collective-permute-start.34 = (f32[1296,128]{1,0:T(8,128)}, f32[1296,128]{1,0:T(8,128)}, u32[]{:S(2)}, u32[]{:S(2)}) collective-permute-start(f32[1296,128]{1,0:T(8,128)} %collective-permute-done.28), channel_id=1, source_target_pairs={{0,3},{1,0},{2,1},{3,2},{4,7},{5,4},{6,5},{7,6},{8,56},{9,57},{10,... | collective-permute-start | bytes 1990664 | tf_op jit(solution)/shard_map/ppermute | solution.py:341
  64.1 7.2 %collective-permute-start.39 = (f32[1296,128]{1,0:T(8,128)S(1)}, f32[1296,128]{1,0:T(8,128)S(1)}, u32[]{:S(2)}, u32[]{:S(2)}) collective-permute-start(f32[1296,128]{1,0:T(8,128)S(1)} %collective-permute-done.26), channel_id=1, source_target_pairs={{0,8},{8,0},{1,9},{9,1},{2,10},{10,2},{3,11},{11,3},{4,12},{12,4},... | collective-permute-start | bytes 1990664 | tf_op jit(solution)/shard_map/ppermute | solution.py:296
  66.3 17.0 %collective-permute-start.41 = (f32[1288,128]{1,0:T(8,128)S(1)}, f32[1288,128]{1,0:T(8,128)S(1)}, u32[]{:S(2)}, u32[]{:S(2)}) collective-permute-start(f32[1288,128]{1,0:T(8,128)S(1)} %add.117), channel_id=1, source_target_pairs={{0,4},{1,5},{2,6},{3,7},{4,0},{5,1},{6,2},{7,3},{8,72},{9,73},{10,... | collective-permute-start | bytes 1978376 | tf_op jit(solution)/shard_map/ppermute | solution.py:341
  71.3 15.7 %collective-permute-start.49 = (f32[1296,128]{1,0:T(8,128)}, f32[1296,128]{1,0:T(8,128)}, u32[]{:S(2)}, u32[]{:S(2)}) collective-permute-start(f32[1296,128]{1,0:T(8,128)} %collective-permute-done.34), channel_id=1, source_target_pairs={{0,3},{1,0},{2,1},{3,2},{4,7},{5,4},{6,5},{7,6},{8,56},{9,57},{10,... | collective-permute-start | bytes 1990664 | tf_op jit(solution)/shard_map/ppermute | solution.py:341
  74.1 11.0 %collective-permute-start.48 = (f32[1280,128]{1,0:T(8,128)S(1)}, f32[1280,128]{1,0:T(8,128)}, u32[]{:S(2)}, u32[]{:S(2)}) collective-permute-start(f32[1280,128]{1,0:T(8,128)S(1)} %collective-permute-done.30), channel_id=1, source_target_pairs={{0,1},{1,2},{2,3},{3,0},{4,5},{5,6},{6,7},{7,4},{8,24},{9,25},{10,... | collective-permute-start | bytes 1966088 | tf_op jit(solution)/shard_map/ppermute | solution.py:341
  74.1 12.3 %collective-permute-start.44 = (f32[1280,128]{1,0:T(8,128)S(1)}, f32[1280,128]{1,0:T(8,128)S(1)}, u32[]{:S(2)}, u32[]{:S(2)}) collective-permute-start(f32[1280,128]{1,0:T(8,128)S(1)} %collective-permute-done.30), channel_id=1, source_target_pairs={{0,8},{8,0},{1,9},{9,1},{2,10},{10,2},{3,11},{11,3},{4,12},{12,4},... | collective-permute-start | bytes 1966088 | tf_op jit(solution)/shard_map/ppermute | solution.py:296
  75.4 11.1 %collective-permute-start.46 = (f32[1280,128]{1,0:T(8,128)S(1)}, f32[1280,128]{1,0:T(8,128)S(1)}, u32[]{:S(2)}, u32[]{:S(2)}) collective-permute-start(f32[1280,128]{1,0:T(8,128)S(1)} %collective-permute-done.31), channel_id=1, source_target_pairs={{0,8},{8,0},{1,9},{9,1},{2,10},{10,2},{3,11},{11,3},{4,12},{12,4},... | collective-permute-start | bytes 1966088 | tf_op jit(solution)/shard_map/ppermute | solution.py:296
  86.4 5.9 %collective-permute-start.45 = (f32[1296,128]{1,0:T(8,128)}, f32[1296,128]{1,0:T(8,128)}, u32[]{:S(2)}, u32[]{:S(2)}) collective-permute-start(f32[1296,128]{1,0:T(8,128)} %collective-permute-done.33), channel_id=1, source_target_pairs={{0,8},{8,0},{1,9},{9,1},{2,10},{10,2},{3,11},{11,3},{4,12},{12,4},... | collective-permute-start | bytes 1990664 | tf_op jit(solution)/shard_map/ppermute | solution.py:296
  86.5 5.8 %collective-permute-start.47 = (f32[1296,128]{1,0:T(8,128)}, f32[1296,128]{1,0:T(8,128)}, u32[]{:S(2)}, u32[]{:S(2)}) collective-permute-start(f32[1296,128]{1,0:T(8,128)} %collective-permute-done.34), channel_id=1, source_target_pairs={{0,8},{8,0},{1,9},{9,1},{2,10},{10,2},{3,11},{11,3},{4,12},{12,4},... | collective-permute-start | bytes 1990664 | tf_op jit(solution)/shard_map/ppermute | solution.py:296
  (24 other events, 291.9 us)
where the time goes:
time: 106 us; the launch traced here: 104 us
  waiting for transfers between devices  48.5 us (46%)
  starting transfers between devices  33.2 us (31%)
  Pallas kernels  17.3 us (16%)
  local copies, waits for them, and re-layouts  2.91 us (3%)
  between operations  1.68 us (2%)
    ppermute x15, waiting for transfers between devices, route(): return lax.ppermute(x, ROW + COL, pairs)  40.6 us
    ppermute x15, starting transfers between devices, swap(): return lax.ppermute(x, axis, [(0, 1), (1, 0)])  17.7 us
    ppermute x15, starting transfers between devices, route(): return lax.ppermute(x, ROW + COL, pairs)  15.5 us
    pallas_call x1, Pallas kernels, product(): pl.pallas_call(functools.partial(product_kernel, shapes, spread), out_sha...  11.3 us
    ppermute x15, waiting for transfers between devices, swap(): return lax.ppermute(x, axis, [(0, 1), (1, 0)])  7.89 us
    pallas_call x1, Pallas kernels, pack(): pl.pallas_call(pack_kernel, out_shape=(jax.ShapeDtypeStruct((ROWS, W), jn...  3.63 us
    pallas_call x1, Pallas kernels, merge(): pl.pallas_call(merge_kernel, out_shape=(jax.ShapeDtypeStruct((ROWS, W), j...  2.35 us
  transfers between devices with their start and end apart: 30, of which 11 were waited for; matrix products, arithmetic and copies ran while one was open for 1% of the time, Pallas kernels for 0%

commit v1 on v0

--- a/solution.py
+++ b/solution.py
@@ -135,10 +135,10 @@
             a_at, b_at = where_ref[1 + n], where_ref[9 + n]
             pair = (parts(lines[2 * n]), parts(lines[2 * n + 1]))
             a_parts, b_parts = pair[side], pair[1 - side]
-            found.append((a_parts[side], a_all.at[pl.ds(a_at * DATA, DATA), :]))
+            found.append((a_parts[side], a_all.at[pl.ds(a_at * DATA, DATA), :], 1 + n))
             found.append((a_parts[2].at[pl.ds(8 * side, 8), :], a_meta.at[pl.ds(a_at * 8, 8), :]))
             for h in range(2):
-                found.append((b_parts[h], b_all.at[pl.ds((b_at * 2 + h) * DATA, DATA), :]))
+                found.append((b_parts[h], b_all.at[pl.ds((b_at * 2 + h) * DATA, DATA), :], 9 + n))
             found.append((b_parts[2], b_meta.at[pl.ds(b_at * 16, 16), :]))
         if not spread:
             e = lines[16]
@@ -151,28 +151,33 @@
                 h = side if n < 16 else 1 - side
                 at = 16 + where_ref[9 + n % 8] * 2 + h
                 found.append((piece[0], b_all.at[pl.ds(at * DATA, DATA), :]))
-        found.sort(key=lambda pair: pair[0].shape[0] >= DATA)
-        small = sum(pair[0].shape[0] < DATA for pair in found)
-        made = [pltpu.make_async_copy(src, dst, sem.at[n]) for n, (src, dst) in enumerate(found)]
-        return made, made[:small], made[small:]
+        found.sort(key=lambda item: item[0].shape[0] >= DATA)
+        made = []
+        for n, item in enumerate(found):
+            tag = item[2] if len(item) == 3 else (0 if item[0].shape[0] >= DATA else -1)
+            made.append((pltpu.make_async_copy(item[0], item[1], sem.at[n]), tag))
+        return made
 
     for side in range(2):
 
         @pl.when(core == side)
         def _():
-            for copy in copies(side)[0]:
+            for copy, _ in copies(side):
                 copy.start()
 
-    def settle(which):
+    def settle(half):
         for side in range(2):
 
             @pl.when(core == side)
             def _():
-                for copy in copies(side)[which]:
-                    copy.wait()
+                for copy, tag in copies(side):
+                    if tag > 0 and half >= 0:
+                        pl.when(where_ref[tag] // 4 == half)(copy.wait)
+                    elif (tag == 0 and half == 0) or (tag < 0 and half < 0):
+                        copy.wait()
 
     acc[...] = jnp.zeros(acc.shape, jnp.float32)
-    settle(1)
+    settle(-1)
 
     def address(piece, rank, pieces):
         rest = pieces * SLOTS + rank - (SLOTS + 1)
@@ -210,20 +215,17 @@
     t0.wait()
     t1.wait()
 
-    def gather(p, total):
-        for n in range(2):
-
-            def one(m, bits):
-                lowest = bits & -bits
-                k = 31 - lax.clz(lowest) + 32 * n
-                list_s[0, total + m] = table_s[k, p]
-                list_s[1, total + m] = p
-                return bits ^ lowest
-
-            found = words_s[8 * n + 1, p]
-            lax.fori_loop(0, found, one, words_s[8 * n, p])
-            total = total + found
-        return total
+    def gather(n, p, total):
+        def one(m, bits):
+            lowest = bits & -bits
+            k = 31 - lax.clz(lowest) + 32 * n
+            list_s[0, total + m] = table_s[k, p]
+            list_s[1, total + m] = p
+            return bits ^ lowest
+
+        found = words_s[8 * n + 1, p]
+        lax.fori_loop(0, found, one, words_s[8 * n, p])
+        return total + found
 
     def term(entry):
         a_at = pl.multiple_of((entry & 65535) * W, W)
@@ -240,23 +242,31 @@
     def place(p):
         return pl.ds(pl.multiple_of(p // 8 * W, W), W), pl.ds(pl.multiple_of(p % 8 * W, W), W)
 
-    total = lax.fori_loop(0, 32, gather, jnp.int32(0))
-    settle(2)
-
-    def four(t, _):
-        terms = [term(list_s[0, 4 * t + n]) for n in range(4)]
-        for n in range(4):
-            rows, cols = place(list_s[1, 4 * t + n])
-            acc[rows, cols] = acc[rows, cols] + terms[n]
-        return 0
-
-    def single(t, _):
-        rows, cols = place(list_s[1, t])
-        acc[rows, cols] = acc[rows, cols] + term(list_s[0, t])
-        return 0
-
-    lax.fori_loop(0, total // 4, four, 0)
-    lax.fori_loop(total // 4 * 4, total, single, 0)
+    begin = jnp.int32(0)
+    middle = lax.fori_loop(0, 32, functools.partial(gather, 0), begin)
+    end = lax.fori_loop(0, 32, functools.partial(gather, 1), middle)
+
+    def add(n, value):
+        rows, cols = place(list_s[1, n])
+        acc[rows, cols] = acc[rows, cols] + value
+
+    for half, (start, stop) in enumerate(((begin, middle), (middle, end))):
+        settle(half)
+        fours = (stop - start) // 4
+
+        def four(t, start):
+            at = start + 4 * t
+            terms = [term(list_s[0, at + n]) for n in range(4)]
+            for n in range(4):
+                add(at + n, terms[n])
+            return start
+
+        def single(t, _):
+            add(t, term(list_s[0, t]))
+            return 0
+
+        lax.fori_loop(0, fours, four, start)
+        lax.fori_loop(start + 4 * fours, stop, single, 0)
     out = pltpu.make_async_copy(acc, out_ref, sem_o)
     out.start()
     out.wait()

time: 106 us -> 106 us (level)
  no operation moved by 1% of the time
where the time goes in v1:
time: 106 us; the launch traced here: 105 us
  waiting for transfers between devices  48.5 us (46%)
  starting transfers between devices  33.3 us (31%)
  Pallas kernels  18.3 us (17%)
  local copies, waits for them, and re-layouts  2.91 us (3%)
  between operations  1.66 us (2%)
    ppermute x15, waiting for transfers between devices, route(): return lax.ppermute(x, ROW + COL, pairs)  40.6 us
    ppermute x15, starting transfers between devices, swap(): return lax.ppermute(x, axis, [(0, 1), (1, 0)])  17.9 us
    ppermute x15, starting transfers between devices, route(): return lax.ppermute(x, ROW + COL, pairs)  15.4 us
    pallas_call x1, Pallas kernels, product(): pl.pallas_call(functools.partial(product_kernel, shapes, spread), out_sha...  12.3 us
    ppermute x15, waiting for transfers between devices, swap(): return lax.ppermute(x, axis, [(0, 1), (1, 0)])  7.91 us
    pallas_call x1, Pallas kernels, pack(): pl.pallas_call(pack_kernel, out_shape=(jax.ShapeDtypeStruct((ROWS, W), jn...  3.67 us
    pallas_call x1, Pallas kernels, merge(): pl.pallas_call(merge_kernel, out_shape=(jax.ShapeDtypeStruct((ROWS, W), j...  2.35 us
  transfers between devices with their start and end apart: 30, of which 11 were waited for; matrix products, arithmetic and copies ran while one was open for 1% of the time, Pallas kernels for 0%

profile of v1, /device:TPU:1, one launch (start us, length us, event | category | flops | bytes accessed | tf_op | source)
XLA Modules:
  0.0 105.1 jit_solution(13364188261965267756)
XLA Ops:
  0.0 3.7 %pack.1 = (f32[2576,128]{1,0:T(8,128)S(1)}, f32[2576,128]{1,0:T(8,128)}) custom-call(s32[1]{0:T(128)} %bitcast.core_ref, s32[4,8]{1,0:T(4,128)} %am_ref.1, s32[4,8]{1,0:T(4,128)} %bm_ref.1, f32[512,1024]{1,0:T(8,128)} %a_ref.1, f32[512,1024]{1,0:T(8,128)} %b_ref.1), custom_call_target="tpu_custom_call" | custom-call | tf_op jit(solution)/shard_map/pack/pallas_call | solution.py:74
  3.7 1.6 %collective-permute-start.22 = (f32[2576,128]{1,0:T(8,128)}, f32[2576,128]{1,0:T(8,128)S(1)}, u32[]{:S(2)}, u32[]{:S(2)}) collective-permute-start(f32[2576,128]{1,0:T(8,128)} %get-tuple-element.295), channel_id=1, source_target_pairs={{0,8},{8,0},{1,9},{9,1},{2,10},{10,2},{3,11},{11,3},{4,12},{12,4},... | collective-permute-start | bytes 3956744 | tf_op jit(solution)/shard_map/ppermute | solution.py:306
  5.2 2.9 %collective-permute-done.22.got_ref = f32[2576,128]{1,0:T(8,128)S(1)} collective-permute-done((f32[2576,128]{1,0:T(8,128)}, f32[2576,128]{1,0:T(8,128)S(1)}, u32[]{:S(2)}, u32[]{:S(2)}) %collective-permute-start.22) | collective-permute-done | bytes 1318944 | tf_op jit(solution)/shard_map/ppermute | solution.py:306
  9.2 2.4 %merge.1 = (f32[2576,128]{1,0:T(8,128)S(1)}, f32[1288,128]{1,0:T(8,128)}) custom-call(s32[1]{0:T(128)} %bitcast.core_ref, f32[2576,128]{1,0:T(8,128)S(1)} %get-tuple-element.294.keep_ref, f32[2576,128]{1,0:T(8,128)} %copy-done.15), custom_call_target="tpu_custom_call" | custom-call | tf_op jit(solution)/shard_map/merge/pallas_call | solution.py:98
  12.9 1.5 %collective-permute-start.24 = (f32[2576,128]{1,0:T(8,128)S(1)}, f32[2576,128]{1,0:T(8,128)S(1)}, u32[]{:S(2)}, u32[]{:S(2)}) collective-permute-start(f32[2576,128]{1,0:T(8,128)S(1)} %get-tuple-element.297), channel_id=1, source_target_pairs={{0,3},{1,0},{2,1},{3,2},{4,7},{5,4},{6,5},{7,6},{8,56},{9,57},{10,... | collective-permute-start | bytes 3956744 | tf_op jit(solution)/shard_map/ppermute | solution.py:351
  14.4 1.7 %collective-permute-start.29 = (f32[1280,128]{1,0:T(8,128)S(1)}, f32[1280,128]{1,0:T(8,128)S(1)}, u32[]{:S(2)}, u32[]{:S(2)}) collective-permute-start(f32[1280,128]{1,0:T(8,128)S(1)} %slice.41), channel_id=1, source_target_pairs={{0,4},{1,5},{2,6},{3,7},{4,0},{5,1},{6,2},{7,3},{8,72},{9,73},{10,... | collective-permute-start | bytes 1966088 | tf_op jit(solution)/shard_map/ppermute | solution.py:351
  16.2 11.1 %collective-permute-done.29 = f32[1280,128]{1,0:T(8,128)S(1)} collective-permute-done((f32[1280,128]{1,0:T(8,128)S(1)}, f32[1280,128]{1,0:T(8,128)S(1)}, u32[]{:S(2)}, u32[]{:S(2)}) %collective-permute-start.29) | collective-permute-done | bytes 655392 | tf_op jit(solution)/shard_map/ppermute | solution.py:351
  27.3 7.2 %collective-permute-start.40 = (f32[1280,128]{1,0:T(8,128)S(1)}, f32[1280,128]{1,0:T(8,128)S(1)}, u32[]{:S(2)}, u32[]{:S(2)}) collective-permute-start(f32[1280,128]{1,0:T(8,128)S(1)} %collective-permute-done.29), channel_id=1, source_target_pairs={{0,8},{8,0},{1,9},{9,1},{2,10},{10,2},{3,11},{11,3},{4,12},{12,4},... | collective-permute-start | bytes 1966088 | tf_op jit(solution)/shard_map/ppermute | solution.py:306
  35.3 2.2 %collective-permute-start.26 = (f32[1296,128]{1,0:T(8,128)S(1)}, f32[1296,128]{1,0:T(8,128)S(1)}, u32[]{:S(2)}, u32[]{:S(2)}) collective-permute-start(f32[1296,128]{1,0:T(8,128)S(1)} %slice.53), channel_id=1, source_target_pairs={{0,3},{1,0},{2,1},{3,2},{4,7},{5,4},{6,5},{7,6},{8,56},{9,57},{10,... | collective-permute-start | bytes 1990664 | tf_op jit(solution)/shard_map/ppermute | solution.py:351
  38.8 6.9 %collective-permute-done.25 = f32[1280,128]{1,0:T(8,128)S(1)} collective-permute-done((f32[1280,128]{1,0:T(8,128)S(1)}, f32[1280,128]{1,0:T(8,128)S(1)}, u32[]{:S(2)}, u32[]{:S(2)}) %collective-permute-start.25) | collective-permute-done | bytes 655392 | tf_op jit(solution)/shard_map/ppermute | solution.py:351
  46.8 6.0 %collective-permute-done.30 = f32[1280,128]{1,0:T(8,128)S(1)} collective-permute-done((f32[1280,128]{1,0:T(8,128)S(1)}, f32[1280,128]{1,0:T(8,128)S(1)}, u32[]{:S(2)}, u32[]{:S(2)}) %collective-permute-start.30) | collective-permute-done | bytes 655392 | tf_op jit(solution)/shard_map/ppermute | solution.py:351
  53.8 1.8 %collective-permute-done.31 = f32[1280,128]{1,0:T(8,128)S(1)} collective-permute-done((f32[1280,128]{1,0:T(8,128)S(1)}, f32[1280,128]{1,0:T(8,128)S(1)}, u32[]{:S(2)}, u32[]{:S(2)}) %collective-permute-start.31) | collective-permute-done | bytes 655392 | tf_op jit(solution)/shard_map/ppermute | solution.py:351
  55.6 1.5 %collective-permute-start.37 = (f32[2576,128]{1,0:T(8,128)S(1)}, f32[2576,128]{1,0:T(8,128)S(1)}, u32[]{:S(2)}, u32[]{:S(2)}) collective-permute-start(f32[2576,128]{1,0:T(8,128)S(1)} %collective-permute-done.24), channel_id=1, source_target_pairs={{0,8},{8,0},{1,9},{9,1},{2,10},{10,2},{3,11},{11,3},{4,12},{12,4},... | collective-permute-start | bytes 3956744 | tf_op jit(solution)/shard_map/ppermute | solution.py:306
  57.8 3.0 %collective-permute-done.38 = f32[1280,128]{1,0:T(8,128)S(1)} collective-permute-done((f32[1280,128]{1,0:T(8,128)S(1)}, f32[1280,128]{1,0:T(8,128)S(1)}, u32[]{:S(2)}, u32[]{:S(2)}) %collective-permute-start.38) | collective-permute-done | bytes 655392 | tf_op jit(solution)/shard_map/ppermute | solution.py:306
  60.7 1.9 %collective-permute-start.34 = (f32[1296,128]{1,0:T(8,128)}, f32[1296,128]{1,0:T(8,128)}, u32[]{:S(2)}, u32[]{:S(2)}) collective-permute-start(f32[1296,128]{1,0:T(8,128)} %collective-permute-done.28), channel_id=1, source_target_pairs={{0,3},{1,0},{2,1},{3,2},{4,7},{5,4},{6,5},{7,6},{8,56},{9,57},{10,... | collective-permute-start | bytes 1990664 | tf_op jit(solution)/shard_map/ppermute | solution.py:351
  62.7 1.4 %collective-permute-done.32 = f32[1288,128]{1,0:T(8,128)S(1)} collective-permute-done((f32[1288,128]{1,0:T(8,128)S(1)}, f32[1288,128]{1,0:T(8,128)S(1)}, u32[]{:S(2)}, u32[]{:S(2)}) %collective-permute-start.32) | collective-permute-done | bytes 659488 | tf_op jit(solution)/shard_map/ppermute | solution.py:351
  64.1 2.0 %collective-permute-start.39 = (f32[1296,128]{1,0:T(8,128)S(1)}, f32[1296,128]{1,0:T(8,128)S(1)}, u32[]{:S(2)}, u32[]{:S(2)}) collective-permute-start(f32[1296,128]{1,0:T(8,128)S(1)} %collective-permute-done.26), channel_id=1, source_target_pairs={{0,8},{8,0},{1,9},{9,1},{2,10},{10,2},{3,11},{11,3},{4,12},{12,4},... | collective-permute-start | bytes 1990664 | tf_op jit(solution)/shard_map/ppermute | solution.py:306
  67.1 4.2 %collective-permute-done.33 = f32[1296,128]{1,0:T(8,128)} collective-permute-done((f32[1296,128]{1,0:T(8,128)}, f32[1296,128]{1,0:T(8,128)}, u32[]{:S(2)}, u32[]{:S(2)}) %collective-permute-start.33) | collective-permute-done | bytes 663584 | tf_op jit(solution)/shard_map/ppermute | solution.py:351
  71.3 2.7 %collective-permute-start.49 = (f32[1296,128]{1,0:T(8,128)}, f32[1296,128]{1,0:T(8,128)}, u32[]{:S(2)}, u32[]{:S(2)}) collective-permute-start(f32[1296,128]{1,0:T(8,128)} %collective-permute-done.34), channel_id=1, source_target_pairs={{0,3},{1,0},{2,1},{3,2},{4,7},{5,4},{6,5},{7,6},{8,56},{9,57},{10,... | collective-permute-start | bytes 1990664 | tf_op jit(solution)/shard_map/ppermute | solution.py:351
  75.3 7.9 %collective-permute-done.41 = f32[1288,128]{1,0:T(8,128)S(1)} collective-permute-done((f32[1288,128]{1,0:T(8,128)S(1)}, f32[1288,128]{1,0:T(8,128)S(1)}, u32[]{:S(2)}, u32[]{:S(2)}) %collective-permute-start.41) | collective-permute-done | bytes 659488 | tf_op jit(solution)/shard_map/ppermute | solution.py:351
  85.1 1.4 %collective-permute-start.43 = (f32[1296,128]{1,0:T(8,128)}, f32[1296,128]{1,0:T(8,128)}, u32[]{:S(2)}, u32[]{:S(2)}) collective-permute-start(f32[1296,128]{1,0:T(8,128)} %collective-permute-done.28), channel_id=1, source_target_pairs={{0,8},{8,0},{1,9},{9,1},{2,10},{10,2},{3,11},{11,3},{4,12},{12,4},... | collective-permute-start | bytes 1990664 | tf_op jit(solution)/shard_map/ppermute | solution.py:306
  90.3 2.0 %collective-permute-done.50 = f32[1280,128]{1,0:T(8,128)} collective-permute-done((f32[1280,128]{1,0:T(8,128)}, f32[1280,128]{1,0:T(8,128)}, u32[]{:S(2)}, u32[]{:S(2)}) %collective-permute-start.50) | collective-permute-done | bytes 655392 | tf_op jit(solution)/shard_map/ppermute | solution.py:306
  92.4 12.5 %conditional.3 = (f32[512,1024]{1,0:T(8,128)}) conditional(s32[]{:T(128)} %convert_element_type.9, (s32[17]{0:T(128)S(1)}, s32[64,128]{0,1:T(8,128)S(1)}, f32[2576,128]{1,0:T(8,128)S(1)}, f32[2576,128]{1,0:T(8,128)}, f32[2576,128]{1,0:T(8,128)}, /*index=5*/f32[2576,128]{1,0:T(8,128)}, f32[2576,128]{1,0:T(8,128)}, f32[2576,128]{1,0:T(8,128)}, ...), branch_computations={%region_0.1_spmd, %region_1.6_spmd} | conditional | flops 983047 | bytes 69534936 | solution.py:434
  92.5 12.3 %product.2 = f32[512,1024]{1,0:T(8,128)} custom-call(s32[17]{0:T(128)S(1)} %get-tuple-element.178.where_ref, s32[64,128]{1,0:T(8,128)S(1)} %copy.9.keep_ref, f32[2576,128]{1,0:T(8,128)S(1)} %get-tuple-element.180.refs_0_, f32[2576,128]{1,0:T(8,128)} %get-tuple-element.181.refs_1_, f32[2576,128]{1,0:T(8,128)} %get-tuple-element.182.refs_2_, ...), custom_call_target="tpu_custom_call" | custom-call | tf_op jit(solution)/shard_map/cond/branch_0_fun/product/pallas_call | solution.py:280
  (88 shorter events, 13.9 us)
Async XLA Ops:
  11.6 23.0 %collective-permute-start.23 = (f32[2576,128]{1,0:T(8,128)S(1)}, f32[2576,128]{1,0:T(8,128)S(1)}, u32[]{:S(2)}, u32[]{:S(2)}) collective-permute-start(f32[2576,128]{1,0:T(8,128)S(1)} %get-tuple-element.297), channel_id=1, source_target_pairs={{0,1},{1,2},{2,3},{3,0},{4,5},{5,6},{6,7},{7,4},{8,24},{9,25},{10,... | collective-permute-start | bytes 3956744 | tf_op jit(solution)/shard_map/ppermute | solution.py:351
  12.9 21.7 %collective-permute-start.24 = (f32[2576,128]{1,0:T(8,128)S(1)}, f32[2576,128]{1,0:T(8,128)S(1)}, u32[]{:S(2)}, u32[]{:S(2)}) collective-permute-start(f32[2576,128]{1,0:T(8,128)S(1)} %get-tuple-element.297), channel_id=1, source_target_pairs={{0,3},{1,0},{2,1},{3,2},{4,7},{5,4},{6,5},{7,6},{8,56},{9,57},{10,... | collective-permute-start | bytes 3956744 | tf_op jit(solution)/shard_map/ppermute | solution.py:351
  14.4 12.9 %collective-permute-start.29 = (f32[1280,128]{1,0:T(8,128)S(1)}, f32[1280,128]{1,0:T(8,128)S(1)}, u32[]{:S(2)}, u32[]{:S(2)}) collective-permute-start(f32[1280,128]{1,0:T(8,128)S(1)} %slice.41), channel_id=1, source_target_pairs={{0,4},{1,5},{2,6},{3,7},{4,0},{5,1},{6,2},{7,3},{8,72},{9,73},{10,... | collective-permute-start | bytes 1966088 | tf_op jit(solution)/shard_map/ppermute | solution.py:351
  16.1 22.1 %collective-permute-start.27 = (f32[1288,128]{1,0:T(8,128)}, f32[1288,128]{1,0:T(8,128)S(1)}, u32[]{:S(2)}, u32[]{:S(2)}) collective-permute-start(f32[1288,128]{1,0:T(8,128)} %get-tuple-element.300), channel_id=1, source_target_pairs={{0,1},{1,0},{2,3},{3,2},{4,5},{5,4},{6,7},{7,6},{8,24},{9,25},{10,... | collective-permute-start | bytes 1978376 | tf_op jit(solution)/shard_map/ppermute | solution.py:351
  27.3 11.2 %collective-permute-start.40 = (f32[1280,128]{1,0:T(8,128)S(1)}, f32[1280,128]{1,0:T(8,128)S(1)}, u32[]{:S(2)}, u32[]{:S(2)}) collective-permute-start(f32[1280,128]{1,0:T(8,128)S(1)} %collective-permute-done.29), channel_id=1, source_target_pairs={{0,8},{8,0},{1,9},{9,1},{2,10},{10,2},{3,11},{11,3},{4,12},{12,4},... | collective-permute-start | bytes 1966088 | tf_op jit(solution)/shard_map/ppermute | solution.py:306
  34.6 11.1 %collective-permute-start.25 = (f32[1280,128]{1,0:T(8,128)S(1)}, f32[1280,128]{1,0:T(8,128)S(1)}, u32[]{:S(2)}, u32[]{:S(2)}) collective-permute-start(f32[1280,128]{1,0:T(8,128)S(1)} %slice.52), channel_id=1, source_target_pairs={{0,1},{1,2},{2,3},{3,0},{4,5},{5,6},{6,7},{7,4},{8,24},{9,25},{10,... | collective-permute-start | bytes 1966088 | tf_op jit(solution)/shard_map/ppermute | solution.py:351
  35.3 11.2 %collective-permute-start.26 = (f32[1296,128]{1,0:T(8,128)S(1)}, f32[1296,128]{1,0:T(8,128)S(1)}, u32[]{:S(2)}, u32[]{:S(2)}) collective-permute-start(f32[1296,128]{1,0:T(8,128)S(1)} %slice.53), channel_id=1, source_target_pairs={{0,3},{1,0},{2,1},{3,2},{4,7},{5,4},{6,5},{7,6},{8,56},{9,57},{10,... | collective-permute-start | bytes 1990664 | tf_op jit(solution)/shard_map/ppermute | solution.py:351
  37.5 20.2 %collective-permute-start.35 = (f32[2576,128]{1,0:T(8,128)S(1)}, f32[2576,128]{1,0:T(8,128)S(1)}, u32[]{:S(2)}, u32[]{:S(2)}) collective-permute-start(f32[2576,128]{1,0:T(8,128)S(1)} %get-tuple-element.297), channel_id=1, source_target_pairs={{0,8},{8,0},{1,9},{9,1},{2,10},{10,2},{3,11},{11,3},{4,12},{12,4},... | collective-permute-start | bytes 3956744 | tf_op jit(solution)/shard_map/ppermute | solution.py:306
  38.2 18.9 %collective-permute-start.28 = (f32[1296,128]{1,0:T(8,128)S(1)}, f32[1296,128]{1,0:T(8,128)}, u32[]{:S(2)}, u32[]{:S(2)}) collective-permute-start(f32[1296,128]{1,0:T(8,128)S(1)} %slice.40), channel_id=1, source_target_pairs={{0,4},{1,5},{2,6},{3,7},{4,0},{5,1},{6,2},{7,3},{8,72},{9,73},{10,... | collective-permute-start | bytes 1990664 | tf_op jit(solution)/shard_map/ppermute | solution.py:351
  38.5 14.3 %collective-permute-start.30 = (f32[1280,128]{1,0:T(8,128)S(1)}, f32[1280,128]{1,0:T(8,128)S(1)}, u32[]{:S(2)}, u32[]{:S(2)}) collective-permute-start(f32[1280,128]{1,0:T(8,128)S(1)} %collective-permute-done.29), channel_id=1, source_target_pairs={{0,1},{1,2},{2,3},{3,0},{4,5},{5,6},{6,7},{7,4},{8,24},{9,25},{10,... | collective-permute-start | bytes 1966088 | tf_op jit(solution)/shard_map/ppermute | solution.py:351
  45.8 9.8 %collective-permute-start.31 = (f32[1280,128]{1,0:T(8,128)S(1)}, f32[1280,128]{1,0:T(8,128)S(1)}, u32[]{:S(2)}, u32[]{:S(2)}) collective-permute-start(f32[1280,128]{1,0:T(8,128)S(1)} %collective-permute-done.29), channel_id=1, source_target_pairs={{0,3},{1,0},{2,1},{3,2},{4,7},{5,4},{6,5},{7,6},{8,56},{9,57},{10,... | collective-permute-start | bytes 1966088 | tf_op jit(solution)/shard_map/ppermute | solution.py:351
  46.5 19.7 %collective-permute-start.36 = (f32[2576,128]{1,0:T(8,128)S(1)}, f32[2576,128]{1,0:T(8,128)S(1)}, u32[]{:S(2)}, u32[]{:S(2)}) collective-permute-start(f32[2576,128]{1,0:T(8,128)S(1)} %collective-permute-done.23), channel_id=1, source_target_pairs={{0,8},{8,0},{1,9},{9,1},{2,10},{10,2},{3,11},{11,3},{4,12},{12,4},... | collective-permute-start | bytes 3956744 | tf_op jit(solution)/shard_map/ppermute | solution.py:306
  52.8 11.3 %collective-permute-start.32 = (f32[1288,128]{1,0:T(8,128)S(1)}, f32[1288,128]{1,0:T(8,128)S(1)}, u32[]{:S(2)}, u32[]{:S(2)}) collective-permute-start(f32[1288,128]{1,0:T(8,128)S(1)} %add.116), channel_id=1, source_target_pairs={{0,2},{1,3},{2,0},{3,1},{4,6},{5,7},{6,4},{7,5},{8,40},{9,41},{10,... | collective-permute-start | bytes 1978376 | tf_op jit(solution)/shard_map/ppermute | solution.py:351
  55.6 11.5 %collective-permute-start.37 = (f32[2576,128]{1,0:T(8,128)S(1)}, f32[2576,128]{1,0:T(8,128)S(1)}, u32[]{:S(2)}, u32[]{:S(2)}) collective-permute-start(f32[2576,128]{1,0:T(8,128)S(1)} %collective-permute-done.24), channel_id=1, source_target_pairs={{0,8},{8,0},{1,9},{9,1},{2,10},{10,2},{3,11},{11,3},{4,12},{12,4},... | collective-permute-start | bytes 3956744 | tf_op jit(solution)/shard_map/ppermute | solution.py:306
  57.7 13.6 %collective-permute-start.33 = (f32[1296,128]{1,0:T(8,128)}, f32[1296,128]{1,0:T(8,128)}, u32[]{:S(2)}, u32[]{:S(2)}) collective-permute-start(f32[1296,128]{1,0:T(8,128)} %collective-permute-done.28), channel_id=1, source_target_pairs={{0,1},{1,2},{2,3},{3,0},{4,5},{5,6},{6,7},{7,4},{8,24},{9,25},{10,... | collective-permute-start | bytes 1990664 | tf_op jit(solution)/shard_map/ppermute | solution.py:351
  60.7 10.5 %collective-permute-start.34 = (f32[1296,128]{1,0:T(8,128)}, f32[1296,128]{1,0:T(8,128)}, u32[]{:S(2)}, u32[]{:S(2)}) collective-permute-start(f32[1296,128]{1,0:T(8,128)} %collective-permute-done.28), channel_id=1, source_target_pairs={{0,3},{1,0},{2,1},{3,2},{4,7},{5,4},{6,5},{7,6},{8,56},{9,57},{10,... | collective-permute-start | bytes 1990664 | tf_op jit(solution)/shard_map/ppermute | solution.py:351
  64.1 7.2 %collective-permute-start.39 = (f32[1296,128]{1,0:T(8,128)S(1)}, f32[1296,128]{1,0:T(8,128)S(1)}, u32[]{:S(2)}, u32[]{:S(2)}) collective-permute-start(f32[1296,128]{1,0:T(8,128)S(1)} %collective-permute-done.26), channel_id=1, source_target_pairs={{0,8},{8,0},{1,9},{9,1},{2,10},{10,2},{3,11},{11,3},{4,12},{12,4},... | collective-permute-start | bytes 1990664 | tf_op jit(solution)/shard_map/ppermute | solution.py:306
  66.2 17.0 %collective-permute-start.41 = (f32[1288,128]{1,0:T(8,128)S(1)}, f32[1288,128]{1,0:T(8,128)S(1)}, u32[]{:S(2)}, u32[]{:S(2)}) collective-permute-start(f32[1288,128]{1,0:T(8,128)S(1)} %add.117), channel_id=1, source_target_pairs={{0,4},{1,5},{2,6},{3,7},{4,0},{5,1},{6,2},{7,3},{8,72},{9,73},{10,... | collective-permute-start | bytes 1978376 | tf_op jit(solution)/shard_map/ppermute | solution.py:351
  71.3 15.8 %collective-permute-start.49 = (f32[1296,128]{1,0:T(8,128)}, f32[1296,128]{1,0:T(8,128)}, u32[]{:S(2)}, u32[]{:S(2)}) collective-permute-start(f32[1296,128]{1,0:T(8,128)} %collective-permute-done.34), channel_id=1, source_target_pairs={{0,3},{1,0},{2,1},{3,2},{4,7},{5,4},{6,5},{7,6},{8,56},{9,57},{10,... | collective-permute-start | bytes 1990664 | tf_op jit(solution)/shard_map/ppermute | solution.py:351
  74.0 11.0 %collective-permute-start.48 = (f32[1280,128]{1,0:T(8,128)S(1)}, f32[1280,128]{1,0:T(8,128)}, u32[]{:S(2)}, u32[]{:S(2)}) collective-permute-start(f32[1280,128]{1,0:T(8,128)S(1)} %collective-permute-done.30), channel_id=1, source_target_pairs={{0,1},{1,2},{2,3},{3,0},{4,5},{5,6},{6,7},{7,4},{8,24},{9,25},{10,... | collective-permute-start | bytes 1966088 | tf_op jit(solution)/shard_map/ppermute | solution.py:351
  74.0 12.5 %collective-permute-start.44 = (f32[1280,128]{1,0:T(8,128)S(1)}, f32[1280,128]{1,0:T(8,128)S(1)}, u32[]{:S(2)}, u32[]{:S(2)}) collective-permute-start(f32[1280,128]{1,0:T(8,128)S(1)} %collective-permute-done.30), channel_id=1, source_target_pairs={{0,8},{8,0},{1,9},{9,1},{2,10},{10,2},{3,11},{11,3},{4,12},{12,4},... | collective-permute-start | bytes 1966088 | tf_op jit(solution)/shard_map/ppermute | solution.py:306
  75.3 11.3 %collective-permute-start.46 = (f32[1280,128]{1,0:T(8,128)S(1)}, f32[1280,128]{1,0:T(8,128)S(1)}, u32[]{:S(2)}, u32[]{:S(2)}) collective-permute-start(f32[1280,128]{1,0:T(8,128)S(1)} %collective-permute-done.31), channel_id=1, source_target_pairs={{0,8},{8,0},{1,9},{9,1},{2,10},{10,2},{3,11},{11,3},{4,12},{12,4},... | collective-permute-start | bytes 1966088 | tf_op jit(solution)/shard_map/ppermute | solution.py:306
  86.5 5.9 %collective-permute-start.45 = (f32[1296,128]{1,0:T(8,128)}, f32[1296,128]{1,0:T(8,128)}, u32[]{:S(2)}, u32[]{:S(2)}) collective-permute-start(f32[1296,128]{1,0:T(8,128)} %collective-permute-done.33), channel_id=1, source_target_pairs={{0,8},{8,0},{1,9},{9,1},{2,10},{10,2},{3,11},{11,3},{4,12},{12,4},... | collective-permute-start | bytes 1990664 | tf_op jit(solution)/shard_map/ppermute | solution.py:306
  86.6 5.8 %collective-permute-start.47 = (f32[1296,128]{1,0:T(8,128)}, f32[1296,128]{1,0:T(8,128)}, u32[]{:S(2)}, u32[]{:S(2)}) collective-permute-start(f32[1296,128]{1,0:T(8,128)} %collective-permute-done.34), channel_id=1, source_target_pairs={{0,8},{8,0},{1,9},{9,1},{2,10},{10,2},{3,11},{11,3},{4,12},{12,4},... | collective-permute-start | bytes 1990664 | tf_op jit(solution)/shard_map/ppermute | solution.py:306
  (24 other events, 292.2 us)

commit v2 on v1

--- a/solution.py
+++ b/solution.py
@@ -252,12 +252,10 @@
 
     for half, (start, stop) in enumerate(((begin, middle), (middle, end))):
         settle(half)
-        fours = (stop - start) // 4
-
-        def four(t, start):
-            at = start + 4 * t
-            terms = [term(list_s[0, at + n]) for n in range(4)]
-            for n in range(4):
+        def several(width, t, start):
+            at = start + width * t
+            terms = [term(list_s[0, at + n]) for n in range(width)]
+            for n in range(width):
                 add(at + n, terms[n])
             return start
 
@@ -265,8 +263,11 @@
             add(t, term(list_s[0, t]))
             return 0
 
-        lax.fori_loop(0, fours, four, start)
-        lax.fori_loop(start + 4 * fours, stop, single, 0)
+        for width in (8, 4):
+            times = (stop - start) // width
+            lax.fori_loop(0, times, functools.partial(several, width), start)
+            start = start + width * times
+        lax.fori_loop(start, stop, single, 0)
     out = pltpu.make_async_copy(acc, out_ref, sem_o)
     out.start()
     out.wait()

time: 106 us -> 105 us (level)
  the two profiles are of different devices: /device:TPU:1 before, /device:TPU:33 now
where the time goes in v2:
time: 105 us; the launch traced here: 103 us
  waiting for transfers between devices  47.1 us (45%)
  starting transfers between devices  33.8 us (32%)
  Pallas kernels  17.4 us (17%)
  local copies, waits for them, and re-layouts  2.91 us (3%)
  between operations  1.69 us (2%)
    ppermute x15, waiting for transfers between devices, route(): return lax.ppermute(x, ROW + COL, pairs)  39 us
    ppermute x15, starting transfers between devices, swap(): return lax.ppermute(x, axis, [(0, 1), (1, 0)])  18.4 us
    ppermute x15, starting transfers between devices, route(): return lax.ppermute(x, ROW + COL, pairs)  15.3 us
    pallas_call x1, Pallas kernels, product(): pl.pallas_call(functools.partial(product_kernel, shapes, spread), out_sha...  11.4 us
    ppermute x15, waiting for transfers between devices, swap(): return lax.ppermute(x, axis, [(0, 1), (1, 0)])  8.09 us
    pallas_call x1, Pallas kernels, pack(): pl.pallas_call(pack_kernel, out_shape=(jax.ShapeDtypeStruct((ROWS, W), jn...  3.66 us
    pallas_call x1, Pallas kernels, merge(): pl.pallas_call(merge_kernel, out_shape=(jax.ShapeDtypeStruct((ROWS, W), j...  2.35 us
  transfers between devices with their start and end apart: 30, of which 12 were waited for; matrix products, arithmetic and copies ran while one was open for 1% of the time, Pallas kernels for 0%

profile of v2, /device:TPU:33, one launch (start us, length us, event | category | flops | bytes accessed | tf_op | source)
XLA Modules:
  0.0 103.2 jit_solution(17948417029909191209)
XLA Ops:
  0.0 3.7 %pack.1 = (f32[2576,128]{1,0:T(8,128)S(1)}, f32[2576,128]{1,0:T(8,128)}) custom-call(s32[1]{0:T(128)} %bitcast.core_ref, s32[4,8]{1,0:T(4,128)} %am_ref.1, s32[4,8]{1,0:T(4,128)} %bm_ref.1, f32[512,1024]{1,0:T(8,128)} %a_ref.1, f32[512,1024]{1,0:T(8,128)} %b_ref.1), custom_call_target="tpu_custom_call" | custom-call | tf_op jit(solution)/shard_map/pack/pallas_call | solution.py:74
  4.4 2.9 %collective-permute-done.22.got_ref = f32[2576,128]{1,0:T(8,128)S(1)} collective-permute-done((f32[2576,128]{1,0:T(8,128)}, f32[2576,128]{1,0:T(8,128)S(1)}, u32[]{:S(2)}, u32[]{:S(2)}) %collective-permute-start.22) | collective-permute-done | bytes 1318944 | tf_op jit(solution)/shard_map/ppermute | solution.py:307
  8.4 2.4 %merge.1 = (f32[2576,128]{1,0:T(8,128)S(1)}, f32[1288,128]{1,0:T(8,128)}) custom-call(s32[1]{0:T(128)} %bitcast.core_ref, f32[2576,128]{1,0:T(8,128)S(1)} %get-tuple-element.294.keep_ref, f32[2576,128]{1,0:T(8,128)} %copy-done.15), custom_call_target="tpu_custom_call" | custom-call | tf_op jit(solution)/shard_map/merge/pallas_call | solution.py:98
  10.7 1.4 %collective-permute-start.23 = (f32[2576,128]{1,0:T(8,128)S(1)}, f32[2576,128]{1,0:T(8,128)S(1)}, u32[]{:S(2)}, u32[]{:S(2)}) collective-permute-start(f32[2576,128]{1,0:T(8,128)S(1)} %get-tuple-element.297), channel_id=1, source_target_pairs={{0,1},{1,2},{2,3},{3,0},{4,5},{5,6},{6,7},{7,4},{8,24},{9,25},{10,... | collective-permute-start | bytes 3956744 | tf_op jit(solution)/shard_map/ppermute | solution.py:352
  12.1 1.5 %collective-permute-start.24 = (f32[2576,128]{1,0:T(8,128)S(1)}, f32[2576,128]{1,0:T(8,128)S(1)}, u32[]{:S(2)}, u32[]{:S(2)}) collective-permute-start(f32[2576,128]{1,0:T(8,128)S(1)} %get-tuple-element.297), channel_id=1, source_target_pairs={{0,3},{1,0},{2,1},{3,2},{4,7},{5,4},{6,5},{7,6},{8,56},{9,57},{10,... | collective-permute-start | bytes 3956744 | tf_op jit(solution)/shard_map/ppermute | solution.py:352
  13.8 13.4 %collective-permute-done.29 = f32[1280,128]{1,0:T(8,128)S(1)} collective-permute-done((f32[1280,128]{1,0:T(8,128)S(1)}, f32[1280,128]{1,0:T(8,128)S(1)}, u32[]{:S(2)}, u32[]{:S(2)}) %collective-permute-start.29) | collective-permute-done | bytes 655392 | tf_op jit(solution)/shard_map/ppermute | solution.py:352
  27.2 5.0 %collective-permute-start.40 = (f32[1280,128]{1,0:T(8,128)S(1)}, f32[1280,128]{1,0:T(8,128)S(1)}, u32[]{:S(2)}, u32[]{:S(2)}) collective-permute-start(f32[1280,128]{1,0:T(8,128)S(1)} %collective-permute-done.29), channel_id=1, source_target_pairs={{0,8},{8,0},{1,9},{9,1},{2,10},{10,2},{3,11},{11,3},{4,12},{12,4},... | collective-permute-start | bytes 1966088 | tf_op jit(solution)/shard_map/ppermute | solution.py:307
  32.3 2.7 %collective-permute-start.26 = (f32[1296,128]{1,0:T(8,128)S(1)}, f32[1296,128]{1,0:T(8,128)S(1)}, u32[]{:S(2)}, u32[]{:S(2)}) collective-permute-start(f32[1296,128]{1,0:T(8,128)S(1)} %slice.53), channel_id=1, source_target_pairs={{0,3},{1,0},{2,1},{3,2},{4,7},{5,4},{6,5},{7,6},{8,56},{9,57},{10,... | collective-permute-start | bytes 1990664 | tf_op jit(solution)/shard_map/ppermute | solution.py:352
  37.7 5.5 %collective-permute-done.25 = f32[1280,128]{1,0:T(8,128)S(1)} collective-permute-done((f32[1280,128]{1,0:T(8,128)S(1)}, f32[1280,128]{1,0:T(8,128)S(1)}, u32[]{:S(2)}, u32[]{:S(2)}) %collective-permute-start.25) | collective-permute-done | bytes 655392 | tf_op jit(solution)/shard_map/ppermute | solution.py:352
  45.9 4.4 %collective-permute-done.30 = f32[1280,128]{1,0:T(8,128)S(1)} collective-permute-done((f32[1280,128]{1,0:T(8,128)S(1)}, f32[1280,128]{1,0:T(8,128)S(1)}, u32[]{:S(2)}, u32[]{:S(2)}) %collective-permute-start.30) | collective-permute-done | bytes 655392 | tf_op jit(solution)/shard_map/ppermute | solution.py:352
  50.8 2.3 %collective-permute-done.31 = f32[1280,128]{1,0:T(8,128)S(1)} collective-permute-done((f32[1280,128]{1,0:T(8,128)S(1)}, f32[1280,128]{1,0:T(8,128)S(1)}, u32[]{:S(2)}, u32[]{:S(2)}) %collective-permute-start.31) | collective-permute-done | bytes 655392 | tf_op jit(solution)/shard_map/ppermute | solution.py:352
  53.1 1.6 %collective-permute-start.37 = (f32[2576,128]{1,0:T(8,128)S(1)}, f32[2576,128]{1,0:T(8,128)S(1)}, u32[]{:S(2)}, u32[]{:S(2)}) collective-permute-start(f32[2576,128]{1,0:T(8,128)S(1)} %collective-permute-done.24), channel_id=1, source_target_pairs={{0,8},{8,0},{1,9},{9,1},{2,10},{10,2},{3,11},{11,3},{4,12},{12,4},... | collective-permute-start | bytes 3956744 | tf_op jit(solution)/shard_map/ppermute | solution.py:307
  55.2 3.1 %collective-permute-done.38 = f32[1280,128]{1,0:T(8,128)S(1)} collective-permute-done((f32[1280,128]{1,0:T(8,128)S(1)}, f32[1280,128]{1,0:T(8,128)S(1)}, u32[]{:S(2)}, u32[]{:S(2)}) %collective-permute-start.38) | collective-permute-done | bytes 655392 | tf_op jit(solution)/shard_map/ppermute | solution.py:307
  58.3 1.8 %collective-permute-start.34 = (f32[1296,128]{1,0:T(8,128)}, f32[1296,128]{1,0:T(8,128)}, u32[]{:S(2)}, u32[]{:S(2)}) collective-permute-start(f32[1296,128]{1,0:T(8,128)} %collective-permute-done.28), channel_id=1, source_target_pairs={{0,3},{1,0},{2,1},{3,2},{4,7},{5,4},{6,5},{7,6},{8,56},{9,57},{10,... | collective-permute-start | bytes 1990664 | tf_op jit(solution)/shard_map/ppermute | solution.py:352
  60.1 1.5 %collective-permute-done.32 = f32[1288,128]{1,0:T(8,128)S(1)} collective-permute-done((f32[1288,128]{1,0:T(8,128)S(1)}, f32[1288,128]{1,0:T(8,128)S(1)}, u32[]{:S(2)}, u32[]{:S(2)}) %collective-permute-start.32) | collective-permute-done | bytes 659488 | tf_op jit(solution)/shard_map/ppermute | solution.py:352
  61.6 2.8 %collective-permute-start.39 = (f32[1296,128]{1,0:T(8,128)S(1)}, f32[1296,128]{1,0:T(8,128)S(1)}, u32[]{:S(2)}, u32[]{:S(2)}) collective-permute-start(f32[1296,128]{1,0:T(8,128)S(1)} %collective-permute-done.26), channel_id=1, source_target_pairs={{0,8},{8,0},{1,9},{9,1},{2,10},{10,2},{3,11},{11,3},{4,12},{12,4},... | collective-permute-start | bytes 1990664 | tf_op jit(solution)/shard_map/ppermute | solution.py:307
  65.6 3.2 %collective-permute-done.33 = f32[1296,128]{1,0:T(8,128)} collective-permute-done((f32[1296,128]{1,0:T(8,128)}, f32[1296,128]{1,0:T(8,128)}, u32[]{:S(2)}, u32[]{:S(2)}) %collective-permute-start.33) | collective-permute-done | bytes 663584 | tf_op jit(solution)/shard_map/ppermute | solution.py:352
  68.8 2.7 %collective-permute-start.49 = (f32[1296,128]{1,0:T(8,128)}, f32[1296,128]{1,0:T(8,128)}, u32[]{:S(2)}, u32[]{:S(2)}) collective-permute-start(f32[1296,128]{1,0:T(8,128)} %collective-permute-done.34), channel_id=1, source_target_pairs={{0,3},{1,0},{2,1},{3,2},{4,7},{5,4},{6,5},{7,6},{8,56},{9,57},{10,... | collective-permute-start | bytes 1990664 | tf_op jit(solution)/shard_map/ppermute | solution.py:352
  71.5 2.2 %collective-permute-start.44 = (f32[1280,128]{1,0:T(8,128)S(1)}, f32[1280,128]{1,0:T(8,128)S(1)}, u32[]{:S(2)}, u32[]{:S(2)}) collective-permute-start(f32[1280,128]{1,0:T(8,128)S(1)} %collective-permute-done.30), channel_id=1, source_target_pairs={{0,8},{8,0},{1,9},{9,1},{2,10},{10,2},{3,11},{11,3},{4,12},{12,4},... | collective-permute-start | bytes 1966088 | tf_op jit(solution)/shard_map/ppermute | solution.py:307
  73.7 7.6 %collective-permute-done.41 = f32[1288,128]{1,0:T(8,128)S(1)} collective-permute-done((f32[1288,128]{1,0:T(8,128)S(1)}, f32[1288,128]{1,0:T(8,128)S(1)}, u32[]{:S(2)}, u32[]{:S(2)}) %collective-permute-start.41) | collective-permute-done | bytes 659488 | tf_op jit(solution)/shard_map/ppermute | solution.py:352
  82.5 3.1 %collective-permute-start.43 = (f32[1296,128]{1,0:T(8,128)}, f32[1296,128]{1,0:T(8,128)}, u32[]{:S(2)}, u32[]{:S(2)}) collective-permute-start(f32[1296,128]{1,0:T(8,128)} %collective-permute-done.28), channel_id=1, source_target_pairs={{0,8},{8,0},{1,9},{9,1},{2,10},{10,2},{3,11},{11,3},{4,12},{12,4},... | collective-permute-start | bytes 1990664 | tf_op jit(solution)/shard_map/ppermute | solution.py:307
  89.4 2.0 %collective-permute-done.50 = f32[1280,128]{1,0:T(8,128)} collective-permute-done((f32[1280,128]{1,0:T(8,128)}, f32[1280,128]{1,0:T(8,128)}, u32[]{:S(2)}, u32[]{:S(2)}) %collective-permute-start.50) | collective-permute-done | bytes 655392 | tf_op jit(solution)/shard_map/ppermute | solution.py:307
  91.5 11.6 %conditional.3 = (f32[512,1024]{1,0:T(8,128)}) conditional(s32[]{:T(128)} %convert_element_type.9, (s32[17]{0:T(128)S(1)}, s32[64,128]{0,1:T(8,128)S(1)}, f32[2576,128]{1,0:T(8,128)S(1)}, f32[2576,128]{1,0:T(8,128)}, f32[2576,128]{1,0:T(8,128)}, /*index=5*/f32[2576,128]{1,0:T(8,128)}, f32[2576,128]{1,0:T(8,128)}, f32[2576,128]{1,0:T(8,128)}, ...), branch_computations={%region_0.1_spmd, %region_1.6_spmd} | conditional | flops 983047 | bytes 69534936 | solution.py:435
  91.5 11.4 %product.2 = f32[512,1024]{1,0:T(8,128)} custom-call(s32[17]{0:T(128)S(1)} %get-tuple-element.178.where_ref, s32[64,128]{1,0:T(8,128)S(1)} %copy.9.keep_ref, f32[2576,128]{1,0:T(8,128)S(1)} %get-tuple-element.180.refs_0_, f32[2576,128]{1,0:T(8,128)} %get-tuple-element.181.refs_1_, f32[2576,128]{1,0:T(8,128)} %get-tuple-element.182.refs_2_, ...), custom_call_target="tpu_custom_call" | custom-call | tf_op jit(solution)/shard_map/cond/branch_0_fun/product/pallas_call | solution.py:281
  (88 shorter events, 13.4 us)
Async XLA Ops:
  10.7 21.4 %collective-permute-start.23 = (f32[2576,128]{1,0:T(8,128)S(1)}, f32[2576,128]{1,0:T(8,128)S(1)}, u32[]{:S(2)}, u32[]{:S(2)}) collective-permute-start(f32[2576,128]{1,0:T(8,128)S(1)} %get-tuple-element.297), channel_id=1, source_target_pairs={{0,1},{1,2},{2,3},{3,0},{4,5},{5,6},{6,7},{7,4},{8,24},{9,25},{10,... | collective-permute-start | bytes 3956744 | tf_op jit(solution)/shard_map/ppermute | solution.py:352
  12.1 20.1 %collective-permute-start.24 = (f32[2576,128]{1,0:T(8,128)S(1)}, f32[2576,128]{1,0:T(8,128)S(1)}, u32[]{:S(2)}, u32[]{:S(2)}) collective-permute-start(f32[2576,128]{1,0:T(8,128)S(1)} %get-tuple-element.297), channel_id=1, source_target_pairs={{0,3},{1,0},{2,1},{3,2},{4,7},{5,4},{6,5},{7,6},{8,56},{9,57},{10,... | collective-permute-start | bytes 3956744 | tf_op jit(solution)/shard_map/ppermute | solution.py:352
  13.6 13.6 %collective-permute-start.29 = (f32[1280,128]{1,0:T(8,128)S(1)}, f32[1280,128]{1,0:T(8,128)S(1)}, u32[]{:S(2)}, u32[]{:S(2)}) collective-permute-start(f32[1280,128]{1,0:T(8,128)S(1)} %slice.41), channel_id=1, source_target_pairs={{0,4},{1,5},{2,6},{3,7},{4,0},{5,1},{6,2},{7,3},{8,72},{9,73},{10,... | collective-permute-start | bytes 1966088 | tf_op jit(solution)/shard_map/ppermute | solution.py:352
  13.7 22.3 %collective-permute-start.27 = (f32[1288,128]{1,0:T(8,128)}, f32[1288,128]{1,0:T(8,128)S(1)}, u32[]{:S(2)}, u32[]{:S(2)}) collective-permute-start(f32[1288,128]{1,0:T(8,128)} %get-tuple-element.300), channel_id=1, source_target_pairs={{0,1},{1,0},{2,3},{3,2},{4,5},{5,4},{6,7},{7,6},{8,24},{9,25},{10,... | collective-permute-start | bytes 1978376 | tf_op jit(solution)/shard_map/ppermute | solution.py:352
  27.2 9.9 %collective-permute-start.40 = (f32[1280,128]{1,0:T(8,128)S(1)}, f32[1280,128]{1,0:T(8,128)S(1)}, u32[]{:S(2)}, u32[]{:S(2)}) collective-permute-start(f32[1280,128]{1,0:T(8,128)S(1)} %collective-permute-done.29), channel_id=1, source_target_pairs={{0,8},{8,0},{1,9},{9,1},{2,10},{10,2},{3,11},{11,3},{4,12},{12,4},... | collective-permute-start | bytes 1966088 | tf_op jit(solution)/shard_map/ppermute | solution.py:307
  32.2 11.0 %collective-permute-start.25 = (f32[1280,128]{1,0:T(8,128)S(1)}, f32[1280,128]{1,0:T(8,128)S(1)}, u32[]{:S(2)}, u32[]{:S(2)}) collective-permute-start(f32[1280,128]{1,0:T(8,128)S(1)} %slice.52), channel_id=1, source_target_pairs={{0,1},{1,2},{2,3},{3,0},{4,5},{5,6},{6,7},{7,4},{8,24},{9,25},{10,... | collective-permute-start | bytes 1966088 | tf_op jit(solution)/shard_map/ppermute | solution.py:352
  32.3 12.2 %collective-permute-start.26 = (f32[1296,128]{1,0:T(8,128)S(1)}, f32[1296,128]{1,0:T(8,128)S(1)}, u32[]{:S(2)}, u32[]{:S(2)}) collective-permute-start(f32[1296,128]{1,0:T(8,128)S(1)} %slice.53), channel_id=1, source_target_pairs={{0,3},{1,0},{2,1},{3,2},{4,7},{5,4},{6,5},{7,6},{8,56},{9,57},{10,... | collective-permute-start | bytes 1990664 | tf_op jit(solution)/shard_map/ppermute | solution.py:352
  35.1 19.7 %collective-permute-start.35 = (f32[2576,128]{1,0:T(8,128)S(1)}, f32[2576,128]{1,0:T(8,128)S(1)}, u32[]{:S(2)}, u32[]{:S(2)}) collective-permute-start(f32[2576,128]{1,0:T(8,128)S(1)} %get-tuple-element.297), channel_id=1, source_target_pairs={{0,8},{8,0},{1,9},{9,1},{2,10},{10,2},{3,11},{11,3},{4,12},{12,4},... | collective-permute-start | bytes 3956744 | tf_op jit(solution)/shard_map/ppermute | solution.py:307
  36.0 18.7 %collective-permute-start.28 = (f32[1296,128]{1,0:T(8,128)S(1)}, f32[1296,128]{1,0:T(8,128)}, u32[]{:S(2)}, u32[]{:S(2)}) collective-permute-start(f32[1296,128]{1,0:T(8,128)S(1)} %slice.40), channel_id=1, source_target_pairs={{0,4},{1,5},{2,6},{3,7},{4,0},{5,1},{6,2},{7,3},{8,72},{9,73},{10,... | collective-permute-start | bytes 1990664 | tf_op jit(solution)/shard_map/ppermute | solution.py:352
  37.1 13.1 %collective-permute-start.30 = (f32[1280,128]{1,0:T(8,128)S(1)}, f32[1280,128]{1,0:T(8,128)S(1)}, u32[]{:S(2)}, u32[]{:S(2)}) collective-permute-start(f32[1280,128]{1,0:T(8,128)S(1)} %collective-permute-done.29), channel_id=1, source_target_pairs={{0,1},{1,2},{2,3},{3,0},{4,5},{5,6},{6,7},{7,4},{8,24},{9,25},{10,... | collective-permute-start | bytes 1966088 | tf_op jit(solution)/shard_map/ppermute | solution.py:352
  43.2 9.8 %collective-permute-start.31 = (f32[1280,128]{1,0:T(8,128)S(1)}, f32[1280,128]{1,0:T(8,128)S(1)}, u32[]{:S(2)}, u32[]{:S(2)}) collective-permute-start(f32[1280,128]{1,0:T(8,128)S(1)} %collective-permute-done.29), channel_id=1, source_target_pairs={{0,3},{1,0},{2,1},{3,2},{4,7},{5,4},{6,5},{7,6},{8,56},{9,57},{10,... | collective-permute-start | bytes 1966088 | tf_op jit(solution)/shard_map/ppermute | solution.py:352
  44.5 20.0 %collective-permute-start.36 = (f32[2576,128]{1,0:T(8,128)S(1)}, f32[2576,128]{1,0:T(8,128)S(1)}, u32[]{:S(2)}, u32[]{:S(2)}) collective-permute-start(f32[2576,128]{1,0:T(8,128)S(1)} %collective-permute-done.23), channel_id=1, source_target_pairs={{0,8},{8,0},{1,9},{9,1},{2,10},{10,2},{3,11},{11,3},{4,12},{12,4},... | collective-permute-start | bytes 3956744 | tf_op jit(solution)/shard_map/ppermute | solution.py:307
  50.2 11.3 %collective-permute-start.32 = (f32[1288,128]{1,0:T(8,128)S(1)}, f32[1288,128]{1,0:T(8,128)S(1)}, u32[]{:S(2)}, u32[]{:S(2)}) collective-permute-start(f32[1288,128]{1,0:T(8,128)S(1)} %add.116), channel_id=1, source_target_pairs={{0,2},{1,3},{2,0},{3,1},{4,6},{5,7},{6,4},{7,5},{8,40},{9,41},{10,... | collective-permute-start | bytes 1978376 | tf_op jit(solution)/shard_map/ppermute | solution.py:352
  53.1 12.5 %collective-permute-start.37 = (f32[2576,128]{1,0:T(8,128)S(1)}, f32[2576,128]{1,0:T(8,128)S(1)}, u32[]{:S(2)}, u32[]{:S(2)}) collective-permute-start(f32[2576,128]{1,0:T(8,128)S(1)} %collective-permute-done.24), channel_id=1, source_target_pairs={{0,8},{8,0},{1,9},{9,1},{2,10},{10,2},{3,11},{11,3},{4,12},{12,4},... | collective-permute-start | bytes 3956744 | tf_op jit(solution)/shard_map/ppermute | solution.py:307
  54.8 13.9 %collective-permute-start.33 = (f32[1296,128]{1,0:T(8,128)}, f32[1296,128]{1,0:T(8,128)}, u32[]{:S(2)}, u32[]{:S(2)}) collective-permute-start(f32[1296,128]{1,0:T(8,128)} %collective-permute-done.28), channel_id=1, source_target_pairs={{0,1},{1,2},{2,3},{3,0},{4,5},{5,6},{6,7},{7,4},{8,24},{9,25},{10,... | collective-permute-start | bytes 1990664 | tf_op jit(solution)/shard_map/ppermute | solution.py:352
  58.3 10.4 %collective-permute-start.34 = (f32[1296,128]{1,0:T(8,128)}, f32[1296,128]{1,0:T(8,128)}, u32[]{:S(2)}, u32[]{:S(2)}) collective-permute-start(f32[1296,128]{1,0:T(8,128)} %collective-permute-done.28), channel_id=1, source_target_pairs={{0,3},{1,0},{2,1},{3,2},{4,7},{5,4},{6,5},{7,6},{8,56},{9,57},{10,... | collective-permute-start | bytes 1990664 | tf_op jit(solution)/shard_map/ppermute | solution.py:352
  61.6 7.2 %collective-permute-start.39 = (f32[1296,128]{1,0:T(8,128)S(1)}, f32[1296,128]{1,0:T(8,128)S(1)}, u32[]{:S(2)}, u32[]{:S(2)}) collective-permute-start(f32[1296,128]{1,0:T(8,128)S(1)} %collective-permute-done.26), channel_id=1, source_target_pairs={{0,8},{8,0},{1,9},{9,1},{2,10},{10,2},{3,11},{11,3},{4,12},{12,4},... | collective-permute-start | bytes 1990664 | tf_op jit(solution)/shard_map/ppermute | solution.py:307
  64.5 16.8 %collective-permute-start.41 = (f32[1288,128]{1,0:T(8,128)S(1)}, f32[1288,128]{1,0:T(8,128)S(1)}, u32[]{:S(2)}, u32[]{:S(2)}) collective-permute-start(f32[1288,128]{1,0:T(8,128)S(1)} %add.117), channel_id=1, source_target_pairs={{0,4},{1,5},{2,6},{3,7},{4,0},{5,1},{6,2},{7,3},{8,72},{9,73},{10,... | collective-permute-start | bytes 1978376 | tf_op jit(solution)/shard_map/ppermute | solution.py:352
  68.8 17.4 %collective-permute-start.49 = (f32[1296,128]{1,0:T(8,128)}, f32[1296,128]{1,0:T(8,128)}, u32[]{:S(2)}, u32[]{:S(2)}) collective-permute-start(f32[1296,128]{1,0:T(8,128)} %collective-permute-done.34), channel_id=1, source_target_pairs={{0,3},{1,0},{2,1},{3,2},{4,7},{5,4},{6,5},{7,6},{8,56},{9,57},{10,... | collective-permute-start | bytes 1990664 | tf_op jit(solution)/shard_map/ppermute | solution.py:352
  71.5 11.0 %collective-permute-start.48 = (f32[1280,128]{1,0:T(8,128)S(1)}, f32[1280,128]{1,0:T(8,128)}, u32[]{:S(2)}, u32[]{:S(2)}) collective-permute-start(f32[1280,128]{1,0:T(8,128)S(1)} %collective-permute-done.30), channel_id=1, source_target_pairs={{0,1},{1,2},{2,3},{3,0},{4,5},{5,6},{6,7},{7,4},{8,24},{9,25},{10,... | collective-permute-start | bytes 1966088 | tf_op jit(solution)/shard_map/ppermute | solution.py:352
  71.5 14.1 %collective-permute-start.44 = (f32[1280,128]{1,0:T(8,128)S(1)}, f32[1280,128]{1,0:T(8,128)S(1)}, u32[]{:S(2)}, u32[]{:S(2)}) collective-permute-start(f32[1280,128]{1,0:T(8,128)S(1)} %collective-permute-done.30), channel_id=1, source_target_pairs={{0,8},{8,0},{1,9},{9,1},{2,10},{10,2},{3,11},{11,3},{4,12},{12,4},... | collective-permute-start | bytes 1966088 | tf_op jit(solution)/shard_map/ppermute | solution.py:307
  73.7 12.0 %collective-permute-start.46 = (f32[1280,128]{1,0:T(8,128)S(1)}, f32[1280,128]{1,0:T(8,128)S(1)}, u32[]{:S(2)}, u32[]{:S(2)}) collective-permute-start(f32[1280,128]{1,0:T(8,128)S(1)} %collective-permute-done.31), channel_id=1, source_target_pairs={{0,8},{8,0},{1,9},{9,1},{2,10},{10,2},{3,11},{11,3},{4,12},{12,4},... | collective-permute-start | bytes 1966088 | tf_op jit(solution)/shard_map/ppermute | solution.py:307
  82.5 6.9 %collective-permute-start.43 = (f32[1296,128]{1,0:T(8,128)}, f32[1296,128]{1,0:T(8,128)}, u32[]{:S(2)}, u32[]{:S(2)}) collective-permute-start(f32[1296,128]{1,0:T(8,128)} %collective-permute-done.28), channel_id=1, source_target_pairs={{0,8},{8,0},{1,9},{9,1},{2,10},{10,2},{3,11},{11,3},{4,12},{12,4},... | collective-permute-start | bytes 1990664 | tf_op jit(solution)/shard_map/ppermute | solution.py:307
  85.6 5.9 %collective-permute-start.45 = (f32[1296,128]{1,0:T(8,128)}, f32[1296,128]{1,0:T(8,128)}, u32[]{:S(2)}, u32[]{:S(2)}) collective-permute-start(f32[1296,128]{1,0:T(8,128)} %collective-permute-done.33), channel_id=1, source_target_pairs={{0,8},{8,0},{1,9},{9,1},{2,10},{10,2},{3,11},{11,3},{4,12},{12,4},... | collective-permute-start | bytes 1990664 | tf_op jit(solution)/shard_map/ppermute | solution.py:307
  (24 other events, 296.8 us)
